TPU v7x, 128 devices: a whole 4x4x4 slice. The times are simulated.
128 devices in a mesh: seq: 16 (over z, y), chan: 8 (over x, core).
Axes of the slice: x: 4, y: 4, z: 4, core: 2. Of those that a mesh axis runs over, the one named last changes fastest.
Arguments:
- tokens: bfloat16 [4096, 1024], P('seq', 'chan'), may hold values from -6 to 6
- in_proj: bfloat16 [1024, 3, 1024], P(None, None, 'chan'), may hold values from -0.1875 to 0.1875
- filter_one: float32 [4096, 1024], P('seq', 'chan'), may hold values from -0.09375 to 0.09375
- filter_two: float32 [4096, 1024], P('seq', 'chan'), may hold values from -0.09375 to 0.09375
- out_grad: float32 [4096, 1024], P('seq', 'chan'), may hold values from -0.75 to 0.75
Outputs:
- output: float32 [4096, 1024], P('seq', 'chan')
- token_grad: float32 [4096, 1024], P('seq', 'chan')
- proj_grad: float32 [1024, 3, 1024], P('seq', None, 'chan')
- filter_one_grad: float32 [4096, 1024], P('seq', 'chan')
- filter_two_grad: float32 [4096, 1024], P('seq', 'chan')
All inputs are finite; a program needn't handle non-finite values.
Results may differ from a plain program's by a relative error of at most 0.0029.
Values may be sent and summed in bfloat16 or wider, within the bound.
A program may use at most 128 MiB of HBM per device.

v0:
```python
import jax
import jax.numpy as jnp
from jax import lax
from jax.sharding import PartitionSpec as P


def from_partner(value, axis, distance):
    return lax.ppermute(value, axis, [(i, i ^ 1 << distance) for i in range(lax.axis_size(axis))])


def phase_mul(spectrum, angle):
    cosine = jnp.cos(angle)
    sine = jnp.sin(angle)
    return jnp.stack(
        [cosine * spectrum[0] - sine * spectrum[1], cosine * spectrum[1] + sine * spectrum[0]]
    )


def complex_mul(first, second):
    return jnp.stack(
        [first[0] * second[0] - first[1] * second[1], first[0] * second[1] + first[1] * second[0]]
    )


def conj_mul(first, second):
    return jnp.stack(
        [first[0] * second[0] + first[1] * second[1], first[1] * second[0] - first[0] * second[1]]
    )


def reversed_index(position, level_count):
    result = jnp.zeros((), jnp.int32)
    for bit_index in range(level_count):
        picked = jnp.bitwise_and(jnp.right_shift(position, bit_index), 1)
        result = jnp.bitwise_or(result, jnp.left_shift(picked, level_count - 1 - bit_index))
    return result


def shards(tokens, in_proj, filter_one, filter_two, out_grad):
    full_tokens = lax.all_gather(tokens, "chan", axis=1, tiled=True)
    projected = jnp.einsum("rd,djc->rjc", full_tokens, in_proj, preferred_element_type=jnp.float32)
    values = projected[:, 0]
    gate_one = projected[:, 1]
    gate_two = projected[:, 2]
    seq_count = lax.axis_size("seq")
    rows = tokens.shape[0]
    position = lax.axis_index("seq")
    length = rows * seq_count
    level_count = seq_count.bit_length() - 1
    highest = lax.Precision.HIGHEST
    row_index = jnp.arange(rows, dtype=jnp.int32)
    global_pos = position * rows + row_index
    twist_angle = jnp.pi * global_pos.astype(jnp.float32) / length
    twist_cos = jnp.cos(twist_angle)[:, None, None]
    twist_sin = jnp.sin(twist_angle)[:, None, None]
    grid = row_index[:, None] * row_index[None, :] % rows
    local_angle = 2.0 * jnp.pi * grid.astype(jnp.float32) / rows
    local_cos = jnp.cos(local_angle)
    local_sin = jnp.sin(local_angle)
    freq_index = reversed_index(position, level_count)
    twiddle = 2.0 * jnp.pi * (row_index * freq_index % length).astype(jnp.float32) / length
    twiddle = twiddle[:, None, None, None]

    def local_dft(spectrum, orient):
        cos_part = jnp.einsum("kr,xrbmc->xkbmc", local_cos, spectrum, precision=highest)
        sin_part = jnp.einsum("kr,xrbmc->xkbmc", local_sin, spectrum, precision=highest)
        return jnp.stack([cos_part[0] - orient * sin_part[1], cos_part[1] + orient * sin_part[0]])

    def cross_forward(spectrum):
        for bit_index in reversed(range(level_count)):
            half_span = 1 << bit_index
            partner = from_partner(spectrum, "seq", bit_index)
            is_upper = jnp.bitwise_and(jnp.right_shift(position, bit_index), 1) == 1
            angle = (
                -jnp.pi * jnp.bitwise_and(position, half_span - 1).astype(jnp.float32) / half_span
            )
            spectrum = jnp.where(is_upper, phase_mul(partner - spectrum, angle), spectrum + partner)
        return spectrum

    def cross_inverse(spectrum):
        for bit_index in range(level_count):
            half_span = 1 << bit_index
            partner = from_partner(spectrum, "seq", bit_index)
            is_upper = jnp.bitwise_and(jnp.right_shift(position, bit_index), 1) == 1
            angle = (
                jnp.pi * jnp.bitwise_and(position, half_span - 1).astype(jnp.float32) / half_span
            )
            lower_new = spectrum + phase_mul(partner, angle)
            upper_new = partner - phase_mul(spectrum, angle)
            spectrum = jnp.where(is_upper, upper_new, lower_new)
        return spectrum

    def to_spectrum(signals):
        stacked = jnp.stack(signals, axis=1)
        real_part = jnp.stack([stacked, stacked * twist_cos], axis=1)
        imag_part = jnp.stack([jnp.zeros_like(stacked), -stacked * twist_sin], axis=1)
        spectrum = cross_forward(jnp.stack([real_part, imag_part]))
        spectrum = phase_mul(spectrum, -twiddle)
        return local_dft(spectrum, -1.0)

    def to_signals(spectrum):
        spectrum = local_dft(spectrum, 1.0)
        spectrum = phase_mul(spectrum, twiddle)
        spectrum = cross_inverse(spectrum)
        even_part = spectrum[:, :, 0]
        odd_part = spectrum[:, :, 1]
        combined = even_part[0] + twist_cos * odd_part[0] - twist_sin * odd_part[1]
        return combined / (2.0 * length)

    first_specs = to_spectrum([values, filter_one, filter_two])
    spec_values = first_specs[:, :, :, 0]
    spec_one = first_specs[:, :, :, 1]
    spec_two = first_specs[:, :, :, 2]
    mixed_one = to_signals(complex_mul(spec_one, spec_values)[:, :, :, None])[:, 0]
    inner = gate_one * mixed_one
    spec_inner = to_spectrum([inner])[:, :, :, 0]
    mixed_two = to_signals(complex_mul(spec_two, spec_inner)[:, :, :, None])[:, 0]
    spread_output = gate_two * mixed_two
    grad_two = out_grad * gate_two
    grad_gate_two = out_grad * mixed_two
    spec_grad_two = to_spectrum([grad_two])[:, :, :, 0]
    second_pair = to_signals(
        jnp.stack([conj_mul(spec_grad_two, spec_two), conj_mul(spec_grad_two, spec_inner)], axis=3)
    )
    grad_inner = second_pair[:, 0]
    grad_one = grad_inner * gate_one
    grad_gate_one = grad_inner * mixed_one
    spec_grad_one = to_spectrum([grad_one])[:, :, :, 0]
    first_pair = to_signals(
        jnp.stack([conj_mul(spec_grad_one, spec_one), conj_mul(spec_grad_one, spec_values)], axis=3)
    )
    results = (
        spread_output,
        first_pair[:, 1],
        second_pair[:, 1],
        first_pair[:, 0],
        grad_gate_one,
        grad_gate_two,
    )
    output, filter_one_grad, filter_two_grad, grad_values, grad_gate_one, grad_gate_two = results
    grad_projected = jnp.stack([grad_values, grad_gate_one, grad_gate_two], axis=1).astype(
        jnp.bfloat16
    )
    token_terms = jnp.einsum(
        "rjc,djc->rd", grad_projected, in_proj, preferred_element_type=jnp.float32
    )
    token_grad = lax.psum_scatter(token_terms, "chan", scatter_dimension=1, tiled=True)
    proj_grad = lax.psum_scatter(
        jnp.einsum("rd,rjc->djc", full_tokens, grad_projected, preferred_element_type=jnp.float32),
        "seq",
        scatter_dimension=0,
        tiled=True,
    )
    return (output, token_grad, proj_grad, filter_one_grad, filter_two_grad)


def solution(mesh):
    in_specs = (
        P("seq", "chan"),
        P(None, None, "chan"),
        P("seq", "chan"),
        P("seq", "chan"),
        P("seq", "chan"),
    )
    out_specs = (
        P("seq", "chan"),
        P("seq", "chan"),
        P("seq", None, "chan"),
        P("seq", "chan"),
        P("seq", "chan"),
    )
    return jax.shard_map(shards, mesh=mesh, in_specs=in_specs, out_specs=out_specs, check_vma=False)
```

profile of v0, /device:TPU:1, one launch (start us, length us, event | category | flops | bytes accessed | tf_op | source)
XLA Modules:
  0.0 712.4 jit_solution(13960086768989284763)
XLA Ops:
  8.1 14.6 %all_gather.3 = bf16[256,1024]{1,0:T(8,128)(2,1)S(1)} all-gather(bf16[256,128]{1,0:T(8,128)(2,1)} %param.5), channel_id=1, replica_groups=mesh['seq'=16,'chan'=8] {'chan'}, dimensions={1}, use_global_device_ids=true | all-gather | bytes 589824 | tf_op jit(solution)/shard_map/all_gather | solution.py:40
  29.5 34.6 %collective-permute-done = f32[2,256,2,3,128]{4,1,3,2,0:T(8,128)} collective-permute-done((f32[2,256,2,3,128]{4,1,3,2,0:T(8,128)}, f32[2,256,2,3,128]{4,1,3,2,0:T(8,128)}, u32[]{:S(2)}, u32[]{:S(2)}) %collective-permute-start) | collective-permute-done | bytes 1572896 | tf_op jit(solution)/shard_map/ppermute | solution.py:8
  74.9 43.2 %collective-permute-done.16 = f32[2,256,2,1,128]{4,1,2,3,0:T(8,128)} collective-permute-done((f32[2,256,2,1,128]{4,1,2,3,0:T(8,128)}, f32[2,256,2,1,128]{4,1,2,3,0:T(8,128)}, u32[]{:S(2)}, u32[]{:S(2)}) %collective-permute-start.16) | collective-permute-done | bytes 524320 | tf_op jit(solution)/shard_map/ppermute | solution.py:8
  137.7 35.9 %collective-permute-done.18 = f32[2,256,2,1,128]{4,1,2,3,0:T(8,128)S(1)} collective-permute-done((f32[2,256,2,1,128]{4,1,2,3,0:T(8,128)S(1)}, f32[2,256,2,1,128]{4,1,2,3,0:T(8,128)S(1)}, u32[]{:S(2)}, u32[]{:S(2)}) %collective-permute-start.18) | collective-permute-done | bytes 524320 | tf_op jit(solution)/shard_map/ppermute | solution.py:8
  180.5 42.3 %collective-permute-done.19 = f32[2,256,2,1,128]{4,1,2,3,0:T(8,128)S(1)} collective-permute-done((f32[2,256,2,1,128]{4,1,2,3,0:T(8,128)S(1)}, f32[2,256,2,1,128]{4,1,2,3,0:T(8,128)S(1)}, u32[]{:S(2)}, u32[]{:S(2)}) %collective-permute-start.19) | collective-permute-done | bytes 524320 | tf_op jit(solution)/shard_map/ppermute | solution.py:8
  244.3 8.4 %collective-permute-done.4 = f32[2,256,2,1,128]{4,1,3,2,0:T(8,128)S(1)} collective-permute-done((f32[2,256,2,1,128]{4,1,3,2,0:T(8,128)S(1)}, f32[2,256,2,1,128]{4,1,3,2,0:T(8,128)S(1)}, u32[]{:S(2)}, u32[]{:S(2)}) %collective-permute-start.4) | collective-permute-done | bytes 524320 | tf_op jit(solution)/shard_map/ppermute | solution.py:8
  279.8 8.2 %collective-permute-done.7 = f32[2,256,2,1,128]{4,1,3,2,0:T(8,128)S(1)} collective-permute-done((f32[2,256,2,1,128]{4,1,3,2,0:T(8,128)S(1)}, f32[2,256,2,1,128]{4,1,3,2,0:T(8,128)S(1)}, u32[]{:S(2)}, u32[]{:S(2)}) %collective-permute-start.7) | collective-permute-done | bytes 524320 | tf_op jit(solution)/shard_map/ppermute | solution.py:8
  291.6 9.9 %collective-permute-done.8 = f32[2,256,2,1,128]{4,1,2,3,0:T(8,128)S(1)} collective-permute-done((f32[2,256,2,1,128]{4,1,2,3,0:T(8,128)S(1)}, f32[2,256,2,1,128]{4,1,2,3,0:T(8,128)S(1)}, u32[]{:S(2)}, u32[]{:S(2)}) %collective-permute-start.8) | collective-permute-done | bytes 524320 | tf_op jit(solution)/shard_map/ppermute | solution.py:8
  301.8 10.5 %collective-permute-done.9 = f32[2,256,2,1,128]{4,1,2,3,0:T(8,128)S(1)} collective-permute-done((f32[2,256,2,1,128]{4,1,2,3,0:T(8,128)S(1)}, f32[2,256,2,1,128]{4,1,2,3,0:T(8,128)S(1)}, u32[]{:S(2)}, u32[]{:S(2)}) %collective-permute-start.9) | collective-permute-done | bytes 524320 | tf_op jit(solution)/shard_map/ppermute | solution.py:8
  327.1 10.3 %collective-permute-done.11 = f32[2,256,2,1,128]{4,1,2,3,0:T(8,128)S(1)} collective-permute-done((f32[2,256,2,1,128]{4,1,2,3,0:T(8,128)S(1)}, f32[2,256,2,1,128]{4,1,2,3,0:T(8,128)S(1)}, u32[]{:S(2)}, u32[]{:S(2)}) %collective-permute-start.11) | collective-permute-done | bytes 524320 | tf_op jit(solution)/shard_map/ppermute | solution.py:8
  349.0 12.3 %collective-permute-done.20 = f32[2,256,2,2,128]{4,1,3,2,0:T(8,128)S(1)} collective-permute-done((f32[2,256,2,2,128]{4,1,3,2,0:T(8,128)S(1)}, f32[2,256,2,2,128]{4,1,3,2,0:T(8,128)S(1)}, u32[]{:S(2)}, u32[]{:S(2)}) %collective-permute-start.20) | collective-permute-done | bytes 1048608 | tf_op jit(solution)/shard_map/ppermute | solution.py:8
  367.0 20.0 %collective-permute-done.21 = f32[2,256,2,2,128]{4,1,3,2,0:T(8,128)S(1)} collective-permute-done((f32[2,256,2,2,128]{4,1,3,2,0:T(8,128)S(1)}, f32[2,256,2,2,128]{4,1,3,2,0:T(8,128)S(1)}, u32[]{:S(2)}, u32[]{:S(2)}) %collective-permute-start.21) | collective-permute-done | bytes 1048608 | tf_op jit(solution)/shard_map/ppermute | solution.py:8
  387.9 13.5 %collective-permute-done.22 = f32[2,256,2,2,128]{4,1,3,2,0:T(8,128)S(1)} collective-permute-done((f32[2,256,2,2,128]{4,1,3,2,0:T(8,128)S(1)}, f32[2,256,2,2,128]{4,1,3,2,0:T(8,128)S(1)}, u32[]{:S(2)}, u32[]{:S(2)}) %collective-permute-start.22) | collective-permute-done | bytes 1048608 | tf_op jit(solution)/shard_map/ppermute | solution.py:8
  402.8 25.1 %collective-permute-done.23 = f32[2,256,2,2,128]{4,1,3,2,0:T(8,128)S(1)} collective-permute-done((f32[2,256,2,2,128]{4,1,3,2,0:T(8,128)S(1)}, f32[2,256,2,2,128]{4,1,3,2,0:T(8,128)S(1)}, u32[]{:S(2)}, u32[]{:S(2)}) %collective-permute-start.23) | collective-permute-done | bytes 1048608 | tf_op jit(solution)/shard_map/ppermute | solution.py:8
  429.4 15.5 %collective-permute-done.24 = f32[2,256,2,1,128]{4,1,2,3,0:T(8,128)S(1)} collective-permute-done((f32[2,256,2,1,128]{4,1,2,3,0:T(8,128)S(1)}, f32[2,256,2,1,128]{4,1,2,3,0:T(8,128)S(1)}, u32[]{:S(2)}, u32[]{:S(2)}) %collective-permute-start.24) | collective-permute-done | bytes 524320 | tf_op jit(solution)/shard_map/ppermute | solution.py:8
  445.2 8.0 %collective-permute-done.25 = f32[2,256,2,1,128]{4,1,2,3,0:T(8,128)S(1)} collective-permute-done((f32[2,256,2,1,128]{4,1,2,3,0:T(8,128)S(1)}, f32[2,256,2,1,128]{4,1,2,3,0:T(8,128)S(1)}, u32[]{:S(2)}, u32[]{:S(2)}) %collective-permute-start.25) | collective-permute-done | bytes 524320 | tf_op jit(solution)/shard_map/ppermute | solution.py:8
  455.1 8.0 %collective-permute-done.26 = f32[2,256,2,1,128]{4,1,2,3,0:T(8,128)S(1)} collective-permute-done((f32[2,256,2,1,128]{4,1,2,3,0:T(8,128)S(1)}, f32[2,256,2,1,128]{4,1,2,3,0:T(8,128)S(1)}, u32[]{:S(2)}, u32[]{:S(2)}) %collective-permute-start.26) | collective-permute-done | bytes 524320 | tf_op jit(solution)/shard_map/ppermute | solution.py:8
  464.4 7.5 %collective-permute-done.27 = f32[2,256,2,1,128]{4,1,2,3,0:T(8,128)S(1)} collective-permute-done((f32[2,256,2,1,128]{4,1,2,3,0:T(8,128)S(1)}, f32[2,256,2,1,128]{4,1,2,3,0:T(8,128)S(1)}, u32[]{:S(2)}, u32[]{:S(2)}) %collective-permute-start.27) | collective-permute-done | bytes 524320 | tf_op jit(solution)/shard_map/ppermute | solution.py:8
  486.2 23.0 %collective-permute-done.12 = f32[2,256,2,1,128]{4,1,3,2,0:T(8,128)S(1)} collective-permute-done((f32[2,256,2,1,128]{4,1,3,2,0:T(8,128)S(1)}, f32[2,256,2,1,128]{4,1,3,2,0:T(8,128)S(1)}, u32[]{:S(2)}, u32[]{:S(2)}) %collective-permute-start.12) | collective-permute-done | bytes 524320 | tf_op jit(solution)/shard_map/ppermute | solution.py:8
  513.0 11.4 %collective-permute-done.13 = f32[2,256,2,1,128]{4,1,3,2,0:T(8,128)S(1)} collective-permute-done((f32[2,256,2,1,128]{4,1,3,2,0:T(8,128)S(1)}, f32[2,256,2,1,128]{4,1,3,2,0:T(8,128)S(1)}, u32[]{:S(2)}, u32[]{:S(2)}) %collective-permute-start.13) | collective-permute-done | bytes 524320 | tf_op jit(solution)/shard_map/ppermute | solution.py:8
  524.9 21.9 %collective-permute-done.29 = f32[2,256,2,2,128]{4,1,3,2,0:T(8,128)S(1)} collective-permute-done((f32[2,256,2,2,128]{4,1,3,2,0:T(8,128)S(1)}, f32[2,256,2,2,128]{4,1,3,2,0:T(8,128)S(1)}, u32[]{:S(2)}, u32[]{:S(2)}) %collective-permute-start.29) | collective-permute-done | bytes 1048608 | tf_op jit(solution)/shard_map/ppermute | solution.py:8
  549.1 13.2 %collective-permute-done.30 = f32[2,256,2,2,128]{4,1,3,2,0:T(8,128)S(1)} collective-permute-done((f32[2,256,2,2,128]{4,1,3,2,0:T(8,128)S(1)}, f32[2,256,2,2,128]{4,1,3,2,0:T(8,128)S(1)}, u32[]{:S(2)}, u32[]{:S(2)}) %collective-permute-start.30) | collective-permute-done | bytes 1048608 | tf_op jit(solution)/shard_map/ppermute | solution.py:8
  571.7 21.7 %collective-permute-done.31 = f32[2,256,2,2,128]{4,1,3,2,0:T(8,128)S(1)} collective-permute-done((f32[2,256,2,2,128]{4,1,3,2,0:T(8,128)S(1)}, f32[2,256,2,2,128]{4,1,3,2,0:T(8,128)S(1)}, u32[]{:S(2)}, u32[]{:S(2)}) %collective-permute-start.31) | collective-permute-done | bytes 1048608 | tf_op jit(solution)/shard_map/ppermute | solution.py:8
  600.9 102.0 %all-reduce.7.cloned.1.call-done = f32[1024,3,128]{2,1,0:T(4,128)} async-done(((f32[1024,3,128]{2,1,0:T(4,128)}), f32[1024,3,128]{2,1,0:T(4,128)}) %all-reduce.7.cloned.1.call-update) | async-done | bytes 1572880
  (292 shorter events, 172.3 us)
Async XLA Ops:
  8.0 694.9 %all-reduce.7.cloned.1.call-start = ((), (), s32[]{:S(2)}) async-start(), calls=%async_computation.2 | async-start | bytes 4194304
  25.6 38.5 %collective-permute-start = (f32[2,256,2,3,128]{4,1,3,2,0:T(8,128)}, f32[2,256,2,3,128]{4,1,3,2,0:T(8,128)}, u32[]{:S(2)}, u32[]{:S(2)}) collective-permute-start(f32[2,256,2,3,128]{4,1,3,2,0:T(8,128)} %pad_maximum_fusion), channel_id=1, source_target_pairs={{0,64},{8,72},{16,80},{24,88},{32,96},{40,104},{48,112},{56,120},{... | collective-permute-start | bytes 4718600 | tf_op jit(solution)/shard_map/ppermute | solution.py:8
  69.0 51.6 %collective-permute-start.1 = (f32[2,256,2,3,128]{4,1,3,2,0:T(8,128)}, f32[2,256,2,3,128]{4,1,3,2,0:T(8,128)}, u32[]{:S(2)}, u32[]{:S(2)}) collective-permute-start(f32[2,256,2,3,128]{4,1,3,2,0:T(8,128)} %maximum_select_fusion), channel_id=1, source_target_pairs={{0,32},{8,40},{16,48},{24,56},{32,0},{40,8},{48,16},{56,24},{64,96... | collective-permute-start | bytes 4718600 | tf_op jit(solution)/shard_map/ppermute | solution.py:8
  71.5 46.7 %collective-permute-start.16 = (f32[2,256,2,1,128]{4,1,2,3,0:T(8,128)}, f32[2,256,2,1,128]{4,1,2,3,0:T(8,128)}, u32[]{:S(2)}, u32[]{:S(2)}) collective-permute-start(f32[2,256,2,1,128]{4,1,2,3,0:T(8,128)} %pad_maximum_fusion.11), channel_id=1, source_target_pairs={{0,64},{8,72},{16,80},{24,88},{32,96},{40,104},{48,112},{56,120},{... | collective-permute-start | bytes 1572872 | tf_op jit(solution)/shard_map/ppermute | solution.py:8
  126.7 47.1 %collective-permute-start.2 = (f32[2,256,2,3,128]{4,1,3,2,0:T(8,128)}, f32[2,256,2,3,128]{4,1,3,2,0:T(8,128)S(1)}, u32[]{:S(2)}, u32[]{:S(2)}) collective-permute-start(f32[2,256,2,3,128]{4,1,3,2,0:T(8,128)} %maximum_select_fusion.1), channel_id=1, source_target_pairs={{0,16},{8,24},{16,0},{24,8},{32,48},{40,56},{48,32},{56,40},{64,80... | collective-permute-start | bytes 4718600 | tf_op jit(solution)/shard_map/ppermute | solution.py:8
  134.6 39.1 %collective-permute-start.18 = (f32[2,256,2,1,128]{4,1,2,3,0:T(8,128)S(1)}, f32[2,256,2,1,128]{4,1,2,3,0:T(8,128)S(1)}, u32[]{:S(2)}, u32[]{:S(2)}) collective-permute-start(f32[2,256,2,1,128]{4,1,2,3,0:T(8,128)S(1)} %bitcast_select_fusion.3), channel_id=1, source_target_pairs={{0,16},{8,24},{16,0},{24,8},{32,48},{40,56},{48,32},{56,40},{64,80... | collective-permute-start | bytes 1572872 | tf_op jit(solution)/shard_map/ppermute | solution.py:8
  178.5 48.4 %collective-permute-start.3 = (f32[2,256,2,3,128]{4,1,3,2,0:T(8,128)S(1)}, f32[2,256,2,3,128]{4,1,3,2,0:T(8,128)}, u32[]{:S(2)}, u32[]{:S(2)}) collective-permute-start(f32[2,256,2,3,128]{4,1,3,2,0:T(8,128)S(1)} %maximum_select_fusion.2), channel_id=1, source_target_pairs={{0,8},{8,0},{16,24},{24,16},{32,40},{40,32},{48,56},{56,48},{64,72... | collective-permute-start | bytes 4718600 | tf_op jit(solution)/shard_map/ppermute | solution.py:8
  179.9 42.9 %collective-permute-start.19 = (f32[2,256,2,1,128]{4,1,2,3,0:T(8,128)S(1)}, f32[2,256,2,1,128]{4,1,2,3,0:T(8,128)S(1)}, u32[]{:S(2)}, u32[]{:S(2)}) collective-permute-start(f32[2,256,2,1,128]{4,1,2,3,0:T(8,128)S(1)} %bitcast_select_fusion.6), channel_id=1, source_target_pairs={{0,8},{8,0},{16,24},{24,16},{32,40},{40,32},{48,56},{56,48},{64,72... | collective-permute-start | bytes 1572872 | tf_op jit(solution)/shard_map/ppermute | solution.py:8
  289.8 11.7 %collective-permute-start.8 = (f32[2,256,2,1,128]{4,1,2,3,0:T(8,128)S(1)}, f32[2,256,2,1,128]{4,1,2,3,0:T(8,128)S(1)}, u32[]{:S(2)}, u32[]{:S(2)}) collective-permute-start(f32[2,256,2,1,128]{4,1,2,3,0:T(8,128)S(1)} %pad_maximum_fusion.8), channel_id=1, source_target_pairs={{0,64},{8,72},{16,80},{24,88},{32,96},{40,104},{48,112},{56,120},{... | collective-permute-start | bytes 1572872 | tf_op jit(solution)/shard_map/ppermute | solution.py:8
  323.6 13.8 %collective-permute-start.11 = (f32[2,256,2,1,128]{4,1,2,3,0:T(8,128)S(1)}, f32[2,256,2,1,128]{4,1,2,3,0:T(8,128)S(1)}, u32[]{:S(2)}, u32[]{:S(2)}) collective-permute-start(f32[2,256,2,1,128]{4,1,2,3,0:T(8,128)S(1)} %bitcast_select_fusion.8), channel_id=1, source_target_pairs={{0,8},{8,0},{16,24},{24,16},{32,40},{40,32},{48,56},{56,48},{64,72... | collective-permute-start | bytes 1572872 | tf_op jit(solution)/shard_map/ppermute | solution.py:8
  346.7 14.6 %collective-permute-start.20 = (f32[2,256,2,2,128]{4,1,3,2,0:T(8,128)S(1)}, f32[2,256,2,2,128]{4,1,3,2,0:T(8,128)S(1)}, u32[]{:S(2)}, u32[]{:S(2)}) collective-permute-start(f32[2,256,2,2,128]{4,1,3,2,0:T(8,128)S(1)} %pad_maximum_fusion.3), channel_id=1, source_target_pairs={{0,8},{8,0},{16,24},{24,16},{32,40},{40,32},{48,56},{56,48},{64,72... | collective-permute-start | bytes 3145736 | tf_op jit(solution)/shard_map/ppermute | solution.py:8
  361.6 25.5 %collective-permute-start.21 = (f32[2,256,2,2,128]{4,1,3,2,0:T(8,128)S(1)}, f32[2,256,2,2,128]{4,1,3,2,0:T(8,128)S(1)}, u32[]{:S(2)}, u32[]{:S(2)}) collective-permute-start(f32[2,256,2,2,128]{4,1,3,2,0:T(8,128)S(1)} %fusion.5), channel_id=1, source_target_pairs={{0,16},{8,24},{16,0},{24,8},{32,48},{40,56},{48,32},{56,40},{64,80... | collective-permute-start | bytes 3145736 | tf_op jit(solution)/shard_map/ppermute | solution.py:8
  387.6 13.7 %collective-permute-start.22 = (f32[2,256,2,2,128]{4,1,3,2,0:T(8,128)S(1)}, f32[2,256,2,2,128]{4,1,3,2,0:T(8,128)S(1)}, u32[]{:S(2)}, u32[]{:S(2)}) collective-permute-start(f32[2,256,2,2,128]{4,1,3,2,0:T(8,128)S(1)} %fusion.6), channel_id=1, source_target_pairs={{0,32},{8,40},{16,48},{24,56},{32,0},{40,8},{48,16},{56,24},{64,96... | collective-permute-start | bytes 3145736 | tf_op jit(solution)/shard_map/ppermute | solution.py:8
  401.8 26.2 %collective-permute-start.23 = (f32[2,256,2,2,128]{4,1,3,2,0:T(8,128)S(1)}, f32[2,256,2,2,128]{4,1,3,2,0:T(8,128)S(1)}, u32[]{:S(2)}, u32[]{:S(2)}) collective-permute-start(f32[2,256,2,2,128]{4,1,3,2,0:T(8,128)S(1)} %fusion.7), channel_id=1, source_target_pairs={{0,64},{8,72},{16,80},{24,88},{32,96},{40,104},{48,112},{56,120},{... | collective-permute-start | bytes 3145736 | tf_op jit(solution)/shard_map/ppermute | solution.py:8
  429.3 15.6 %collective-permute-start.24 = (f32[2,256,2,1,128]{4,1,2,3,0:T(8,128)S(1)}, f32[2,256,2,1,128]{4,1,2,3,0:T(8,128)S(1)}, u32[]{:S(2)}, u32[]{:S(2)}) collective-permute-start(f32[2,256,2,1,128]{4,1,2,3,0:T(8,128)S(1)} %pad_maximum_fusion.12), channel_id=1, source_target_pairs={{0,64},{8,72},{16,80},{24,88},{32,96},{40,104},{48,112},{56,120},{... | collective-permute-start | bytes 1572872 | tf_op jit(solution)/shard_map/ppermute | solution.py:8
  484.3 26.4 %collective-permute-start.28 = (f32[2,256,2,2,128]{4,1,3,2,0:T(8,128)S(1)}, f32[2,256,2,2,128]{4,1,3,2,0:T(8,128)S(1)}, u32[]{:S(2)}, u32[]{:S(2)}) collective-permute-start(f32[2,256,2,2,128]{4,1,3,2,0:T(8,128)S(1)} %pad_maximum_fusion.5), channel_id=1, source_target_pairs={{0,8},{8,0},{16,24},{24,16},{32,40},{40,32},{48,56},{56,48},{64,72... | collective-permute-start | bytes 3145736 | tf_op jit(solution)/shard_map/ppermute | solution.py:8
  485.4 23.9 %collective-permute-start.12 = (f32[2,256,2,1,128]{4,1,3,2,0:T(8,128)S(1)}, f32[2,256,2,1,128]{4,1,3,2,0:T(8,128)S(1)}, u32[]{:S(2)}, u32[]{:S(2)}) collective-permute-start(f32[2,256,2,1,128]{4,1,3,2,0:T(8,128)S(1)} %pad_maximum_fusion.10), channel_id=1, source_target_pairs={{0,8},{8,0},{16,24},{24,16},{32,40},{40,32},{48,56},{56,48},{64,72... | collective-permute-start | bytes 1572872 | tf_op jit(solution)/shard_map/ppermute | solution.py:8
  509.5 14.9 %collective-permute-start.13 = (f32[2,256,2,1,128]{4,1,3,2,0:T(8,128)S(1)}, f32[2,256,2,1,128]{4,1,3,2,0:T(8,128)S(1)}, u32[]{:S(2)}, u32[]{:S(2)}) collective-permute-start(f32[2,256,2,1,128]{4,1,3,2,0:T(8,128)S(1)} %fusion.22), channel_id=1, source_target_pairs={{0,16},{8,24},{16,0},{24,8},{32,48},{40,56},{48,32},{56,40},{64,80... | collective-permute-start | bytes 1572872 | tf_op jit(solution)/shard_map/ppermute | solution.py:8
  511.0 35.9 %collective-permute-start.29 = (f32[2,256,2,2,128]{4,1,3,2,0:T(8,128)S(1)}, f32[2,256,2,2,128]{4,1,3,2,0:T(8,128)S(1)}, u32[]{:S(2)}, u32[]{:S(2)}) collective-permute-start(f32[2,256,2,2,128]{4,1,3,2,0:T(8,128)S(1)} %fusion.9), channel_id=1, source_target_pairs={{0,16},{8,24},{16,0},{24,8},{32,48},{40,56},{48,32},{56,40},{64,80... | collective-permute-start | bytes 3145736 | tf_op jit(solution)/shard_map/ppermute | solution.py:8
  524.7 22.9 %collective-permute-start.14 = (f32[2,256,2,1,128]{4,1,3,2,0:T(8,128)S(1)}, f32[2,256,2,1,128]{4,1,3,2,0:T(8,128)S(1)}, u32[]{:S(2)}, u32[]{:S(2)}) collective-permute-start(f32[2,256,2,1,128]{4,1,3,2,0:T(8,128)S(1)} %fusion.23), channel_id=1, source_target_pairs={{0,32},{8,40},{16,48},{24,56},{32,0},{40,8},{48,16},{56,24},{64,96... | collective-permute-start | bytes 1572872 | tf_op jit(solution)/shard_map/ppermute | solution.py:8
  547.5 14.8 %collective-permute-start.30 = (f32[2,256,2,2,128]{4,1,3,2,0:T(8,128)S(1)}, f32[2,256,2,2,128]{4,1,3,2,0:T(8,128)S(1)}, u32[]{:S(2)}, u32[]{:S(2)}) collective-permute-start(f32[2,256,2,2,128]{4,1,3,2,0:T(8,128)S(1)} %fusion.10), channel_id=1, source_target_pairs={{0,32},{8,40},{16,48},{24,56},{32,0},{40,8},{48,16},{56,24},{64,96... | collective-permute-start | bytes 3145736 | tf_op jit(solution)/shard_map/ppermute | solution.py:8
  547.8 23.4 %collective-permute-start.15 = (f32[2,256,2,1,128]{4,1,3,2,0:T(8,128)S(1)}, f32[2,256,2,1,128]{4,1,3,2,0:T(8,128)S(1)}, u32[]{:S(2)}, u32[]{:S(2)}) collective-permute-start(f32[2,256,2,1,128]{4,1,3,2,0:T(8,128)S(1)} %fusion.24), channel_id=1, source_target_pairs={{0,64},{8,72},{16,80},{24,88},{32,96},{40,104},{48,112},{56,120},{... | collective-permute-start | bytes 1572872 | tf_op jit(solution)/shard_map/ppermute | solution.py:8
  562.7 30.7 %collective-permute-start.31 = (f32[2,256,2,2,128]{4,1,3,2,0:T(8,128)S(1)}, f32[2,256,2,2,128]{4,1,3,2,0:T(8,128)S(1)}, u32[]{:S(2)}, u32[]{:S(2)}) collective-permute-start(f32[2,256,2,2,128]{4,1,3,2,0:T(8,128)S(1)} %fusion.11), channel_id=1, source_target_pairs={{0,64},{8,72},{16,80},{24,88},{32,96},{40,104},{48,112},{56,120},{... | collective-permute-start | bytes 3145736 | tf_op jit(solution)/shard_map/ppermute | solution.py:8
  596.8 107.7 %reduce-scatter.2.cloned.1.call-start = ((), (), s32[]{:S(2)}) async-start(), calls=%async_computation.1 | async-start | bytes 1179648 | tf_op jit(solution)/shard_map/reduce_scatter | solution.py:147
  (46 other events, 413.5 us)
Sparse Core Ops, SparseCore 0:
  596.9 105.9 all-reduce.6
Sparse Core Ops, SparseCore 1:
  600.2 46.3 reduce-scatter.1
where the time goes:
time: 719 us; the launch traced here: 712 us
  waiting for transfers between devices  537 us (75%)
  starting transfers between devices  50.3 us (7%)
  other arithmetic  45.9 us (6%)
  matrix products  35.4 us (5%)
  between operations  19 us (3%)
  blocking collectives  14.6 us (2%)
  local copies, waits for them, and re-layouts  9.81 us (1%)
    ppermute x32, waiting for transfers between devices, from_partner(): lax.ppermute(value, axis, [(i, i ^ 1 << distance) for i in range(lax.axis...  435 us
    unnamed x3, waiting for transfers between devices  102 us
    ppermute x32, starting transfers between devices, from_partner(): lax.ppermute(value, axis, [(i, i ^ 1 << distance) for i in range(lax.axis...  50.2 us
    dot_general x8, matrix products, local_dft(): jnp.einsum('kr,xrbmc->xkbmc', local_sin, spectrum, precision=highest)  16.8 us
    dot_general x8, matrix products, local_dft(): jnp.einsum('kr,xrbmc->xkbmc', local_cos, spectrum, precision=highest)  16.3 us
    all_gather x1, blocking collectives, shards(): full_tokens = lax.all_gather(tokens, 'chan', axis=1, tiled=True)  14.6 us
  transfers between devices with their start and end apart: 34, of which 28 were waited for; matrix products, arithmetic and copies ran while one was open for 4% of the time, Pallas kernels for 0%

commit v1 on v0

v1 whole, which is shorter than its diff:
```python
import functools

import jax
import jax.numpy as jnp
import numpy as np
from jax import lax
from jax.experimental import pallas as pl
from jax.experimental.pallas import tpu as pltpu
from jax.sharding import PartitionSpec as P

OUTER = 32
INNER = 128
LENGTH = OUTER * INNER
CH = 8
ROWS = OUTER * CH
BF16 = jnp.bfloat16
F32 = jnp.float32


def split_const(matrix):
    high = matrix.astype(np.float32).astype(BF16)
    low = (matrix - high.astype(np.float64)).astype(np.float32).astype(BF16)
    return high, low


def tables():
    outer = np.arange(OUTER)
    inner = np.arange(INNER)
    shifted = outer + 0.25
    theta = 2 * np.pi * np.outer(shifted, outer) / OUTER
    eye = np.eye(CH)
    forward = np.concatenate([np.kron(np.cos(theta), eye), np.kron(-np.sin(theta), eye)], axis=0)
    backward = np.concatenate([np.kron(np.cos(theta.T), eye), np.kron(-np.sin(theta.T), eye)], axis=1) / LENGTH
    psi = 2 * np.pi * (np.outer(inner, inner) % INNER) / INNER
    cos, sin = np.cos(psi), np.sin(psi)
    dft = np.block([[cos, -sin], [sin, cos]])
    idft = np.block([[cos, sin], [-sin, cos]])
    phi = np.repeat(2 * np.pi * np.outer(shifted, inner) / LENGTH, CH, axis=0)
    high, low = split_const(forward)
    fwd = np.concatenate([high, low, high], axis=1)
    high, low = split_const(backward)
    bwd = np.concatenate([high, low, high], axis=1)
    high, low = split_const(dft)
    dft3 = np.concatenate([high, low, high], axis=0)
    high, low = split_const(idft)
    idft3 = np.concatenate([high, low, high], axis=0)
    twiddle = np.stack([np.cos(phi), np.sin(phi)]).astype(np.float32)
    return fwd, bwd, dft3, idft3, twiddle


def halves(value):
    high = value.astype(BF16)
    low = (value - high.astype(F32)).astype(BF16)
    return high, low


def product(left, right):
    return jnp.dot(left, right, preferred_element_type=F32)


def to_spectra(signals, fwd_ref, dft_ref, cos, sin):
    high, low = halves(jnp.concatenate(signals, axis=1))
    stage = product(fwd_ref[...], jnp.concatenate([high, high, low], axis=0))
    rows = []
    for n in range(len(signals)):
        real = stage[:ROWS, n * INNER : (n + 1) * INNER]
        imag = stage[ROWS:, n * INNER : (n + 1) * INNER]
        rows.append(jnp.concatenate([real * cos + imag * sin, imag * cos - real * sin], axis=1))
    high, low = halves(jnp.concatenate(rows, axis=0))
    out = product(jnp.concatenate([high, high, low], axis=1), dft_ref[...])
    return [
        (out[n * ROWS : (n + 1) * ROWS, :INNER], out[n * ROWS : (n + 1) * ROWS, INNER:])
        for n in range(len(signals))
    ]


def to_signals(spectra, bwd_ref, idft_ref, cos, sin):
    stacked = jnp.concatenate([jnp.concatenate(pair, axis=1) for pair in spectra], axis=0)
    high, low = halves(stacked)
    out = product(jnp.concatenate([high, high, low], axis=1), idft_ref[...])
    columns = []
    for n in range(len(spectra)):
        real = out[n * ROWS : (n + 1) * ROWS, :INNER]
        imag = out[n * ROWS : (n + 1) * ROWS, INNER:]
        columns.append(jnp.concatenate([real * cos - imag * sin, imag * cos + real * sin], axis=0))
    high, low = halves(jnp.concatenate(columns, axis=1))
    signals = product(bwd_ref[...], jnp.concatenate([high, high, low], axis=0))
    return [signals[:, n * INNER : (n + 1) * INNER] for n in range(len(spectra))]


def times(first, second):
    return first[0] * second[0] - first[1] * second[1], first[0] * second[1] + first[1] * second[0]


def times_conj(first, second):
    return first[0] * second[0] + first[1] * second[1], first[1] * second[0] - first[0] * second[1]


def local_kernel(sig_ref, fwd_ref, bwd_ref, dft_ref, idft_ref, twiddle_ref, out_ref, grad_ref):
    cos, sin = twiddle_ref[0], twiddle_ref[1]
    values, gate_one, gate_two, filter_one, filter_two, out_grad = [sig_ref[n] for n in range(6)]
    grad_two = out_grad * gate_two
    spec_values, spec_one, spec_two, spec_grad_two = to_spectra(
        [values, filter_one, filter_two, grad_two], fwd_ref, dft_ref, cos, sin
    )
    mixed_one, grad_inner = to_signals(
        [times(spec_one, spec_values), times_conj(spec_grad_two, spec_two)], bwd_ref, idft_ref, cos, sin
    )
    inner = gate_one * mixed_one
    grad_one = grad_inner * gate_one
    spec_inner, spec_grad_one = to_spectra([inner, grad_one], fwd_ref, dft_ref, cos, sin)
    mixed_two, filter_two_grad, grad_values, filter_one_grad = to_signals(
        [
            times(spec_two, spec_inner),
            times_conj(spec_grad_two, spec_inner),
            times_conj(spec_grad_one, spec_one),
            times_conj(spec_grad_one, spec_values),
        ],
        bwd_ref,
        idft_ref,
        cos,
        sin,
    )
    out_ref[0] = gate_two * mixed_two
    out_ref[1] = filter_one_grad
    out_ref[2] = filter_two_grad
    grad_ref[0] = grad_values.astype(BF16)
    grad_ref[1] = (grad_inner * mixed_one).astype(BF16)
    grad_ref[2] = (out_grad * mixed_two).astype(BF16)


def local_part(signals):
    vmem = pl.BlockSpec(memory_space=pltpu.VMEM)
    return pl.pallas_call(
        local_kernel,
        out_shape=(
            jax.ShapeDtypeStruct((3, ROWS, INNER), F32),
            jax.ShapeDtypeStruct((3, ROWS, INNER), BF16),
        ),
        in_specs=[vmem] * 6,
        out_specs=(vmem, vmem),
        name="local_chain",
    )(signals, *[jnp.asarray(t) for t in tables()])


def shards(tokens, in_proj, filter_one, filter_two, out_grad):
    seq = lax.axis_size("seq")
    rows, width = tokens.shape
    full_tokens = lax.all_gather(tokens, "chan", axis=1, tiled=True)
    projected = jnp.einsum("rd,djc->jrc", full_tokens, in_proj, preferred_element_type=F32)
    stacked = jnp.concatenate([projected, jnp.stack([filter_one, filter_two, out_grad])], axis=0)
    blocks = stacked.reshape(6, rows, seq, CH).transpose(2, 0, 3, 1).reshape(seq, 6, CH, rows // INNER, INNER)
    arrived = lax.all_to_all(blocks.transpose(0, 1, 3, 2, 4), "seq", 0, 0)
    signals = arrived.transpose(1, 0, 2, 3, 4).reshape(6, ROWS, INNER)
    outs, grads = local_part(signals)

    def back(array):
        parted = array.reshape(3, seq, rows // INNER, CH, INNER).transpose(1, 0, 2, 3, 4)
        home = lax.all_to_all(parted, "seq", 0, 0)
        return home.transpose(1, 2, 4, 0, 3).reshape(3, rows, width)

    outs = back(outs)
    grads = back(grads)
    token_terms = jnp.einsum("jrc,djc->rd", grads, in_proj, preferred_element_type=F32)
    token_grad = lax.psum_scatter(token_terms, "chan", scatter_dimension=1, tiled=True)
    proj_grad = lax.psum_scatter(
        jnp.einsum("rd,jrc->djc", full_tokens, grads, preferred_element_type=F32),
        "seq",
        scatter_dimension=0,
        tiled=True,
    )
    return outs[0], token_grad, proj_grad, outs[1], outs[2]


def solution(mesh):
    in_specs = (
        P("seq", "chan"),
        P(None, None, "chan"),
        P("seq", "chan"),
        P("seq", "chan"),
        P("seq", "chan"),
    )
    out_specs = (
        P("seq", "chan"),
        P("seq", "chan"),
        P("seq", None, "chan"),
        P("seq", "chan"),
        P("seq", "chan"),
    )
    return jax.shard_map(shards, mesh=mesh, in_specs=in_specs, out_specs=out_specs, check_vma=False)
```

time: 719 us -> 171 us (0.24)
  waiting for transfers between devices: 537 us -> 81.2 us
  starting transfers between devices: 50.3 us -> 3.63 us
  other arithmetic: 45.9 us -> 0.06 us
  matrix products: 35.4 us -> 2.23 us
  blocking collectives: 14.6 us -> 46.2 us
  Pallas kernels: 0 us -> 7.75 us
    ppermute x32 -> x0, waiting for transfers between devices: 435 us -> none  [from_partner(): lax.ppermute(value, axis, [(i, i ^ 1 << distance) for i in range(lax.axis...]
    ppermute x32 -> x0, starting transfers between devices: 50.2 us -> none  [from_partner(): lax.ppermute(value, axis, [(i, i ^ 1 << distance) for i in range(lax.axis...]
    dot_general x19 -> x3, matrix products: 35.4 us -> 2.23 us  [the longest x1 1.44 us: shards(): jnp.einsum('jrc,djc->rd', grads, in_proj, preferred_element_type=F32)]
    unnamed x3, waiting for transfers between devices: 102 us -> 69.3 us
    all_to_all x0 -> x2, blocking collectives: none -> 31.8 us  [the longest x1 21.6 us: shards(): arrived = lax.all_to_all(blocks.transpose(0, 1, 3, 2, 4), 'seq', 0, 0)]
    select_n x32 -> x0, other arithmetic: 21.4 us -> none  [the longest x16 14 us: cross_forward(): jnp.where(is_upper, phase_mul(partner - spectrum, angle), spectrum + part...]
    sub x72 -> x0, other arithmetic: 17.5 us -> none  [the longest x16 10.5 us: cross_forward(): partner - spectrum]
    all_to_all x0 -> x1, waiting for transfers between devices: none -> 11.9 us  [back(): home = lax.all_to_all(parted, 'seq', 0, 0)]
  transfers between devices with their start and end apart: 34 -> 3, of which waited for: 28 -> 2; matrix products, arithmetic and copies ran while one was open for 4% -> 4% of each run, Pallas kernels for 0% -> 0%
where the time goes in v1:
time: 171 us; the launch traced here: 170 us
  waiting for transfers between devices  81.2 us (47%)
  blocking collectives  46.2 us (27%)
  between operations  16.3 us (10%)
  local copies, waits for them, and re-layouts  12.6 us (7%)
  Pallas kernels  7.75 us (5%)
  starting transfers between devices  3.63 us (2%)
  matrix products  2.23 us (1%)
    unnamed x3, waiting for transfers between devices  69.3 us
    all_to_all x1, blocking collectives, shards(): arrived = lax.all_to_all(blocks.transpose(0, 1, 3, 2, 4), 'seq', 0, 0)  21.6 us
    all_gather x1, blocking collectives, shards(): full_tokens = lax.all_gather(tokens, 'chan', axis=1, tiled=True)  14.5 us
    all_to_all x1, waiting for transfers between devices, back(): home = lax.all_to_all(parted, 'seq', 0, 0)  11.9 us
    all_to_all x1, blocking collectives, back(): home = lax.all_to_all(parted, 'seq', 0, 0)  10.2 us
    pallas_call x1, Pallas kernels, local_part(): pl.pallas_call(local_kernel, out_shape=(jax.ShapeDtypeStruct((3, ROWS, IN...  7.75 us
    unnamed x17, local copies, waits for them, and re-layouts  7.54 us
    all_to_all x1, starting transfers between devices, back(): home = lax.all_to_all(parted, 'seq', 0, 0)  3.55 us
  transfers between devices with their start and end apart: 3, of which 2 were waited for; matrix products, arithmetic and copies ran while one was open for 4% of the time, Pallas kernels for 0%

profile of v1, /device:TPU:1, one launch (start us, length us, event | category | flops | bytes accessed | tf_op | source)
XLA Modules:
  0.0 170.0 jit_solution(8597749101426197000)
XLA Ops:
  8.1 1.1 copy.53
  9.1 1.0 copy.52
  10.1 1.0 copy.51
  11.1 14.5 %all_gather.3 = bf16[256,1024]{1,0:T(8,128)(2,1)S(1)} all-gather(bf16[256,128]{1,0:T(8,128)(2,1)} %param.10), channel_id=1, replica_groups=mesh['seq'=16,'chan'=8] {'chan'}, dimensions={1}, use_global_device_ids=true | all-gather | bytes 589824 | tf_op jit(solution)/shard_map/all_gather | solution.py:149
  25.6 0.4 convolution_bitcast_fusion.2
  26.1 21.6 %all_to_all.15 = f32[16,6,2,8,128]{4,3,2,1,0:T(8,128)S(1)} all-to-all(f32[16,6,2,8,128]{4,3,2,1,0:T(8,128)S(1)} %maximum_bitcast_fusion), channel_id=1, replica_groups=mesh['seq'=16,'chan'=8] {'seq'}, dimensions={0} | all-to-all | bytes 1572864 | tf_op jit(solution)/shard_map/all_to_all | solution.py:153
  47.7 1.0 copy.58
  48.6 7.8 %local_chain.1 = (f32[3,256,128]{2,1,0:T(8,128)}, bf16[3,256,128]{2,1,0:T(8,128)(2,1)}) custom-call(f32[6,256,128]{2,1,0:T(8,128)} %bitcast.70, bf16[512,768]{1,0:T(8,128)(2,1)} %constant.10.clone.fwd_ref, bf16[256,1536]{1,0:T(8,128)(2,1)} %constant.11.clone.bwd_ref, bf16[768,256]{1,0:T(8,128)(2,1)} %constant.12.clone.dft_ref, ...), custom_call_target="tpu_custom_call" | custom-call | tf_op jit(solution)/shard_map/local_chain/pallas_call | solution.py:134
  56.4 1.1 copy.81
  57.5 10.2 %all_to_all.16 = bf16[16,3,2,8,128]{4,2,3,1,0:T(2,128)(2,1)S(1)} all-to-all(bf16[16,3,2,8,128]{4,2,3,1,0:T(2,128)(2,1)S(1)} %bitcast.72), channel_id=1, replica_groups=mesh['seq'=16,'chan'=8] {'seq'}, dimensions={0} | all-to-all | bytes 393216 | tf_op jit(solution)/shard_map/all_to_all | solution.py:159
  67.7 0.1 copy.61
  67.9 0.4 convolution_bitcast_fusion
  68.3 1.8 %copy.63 = f32[1024,3,128]{2,1,0:T(4,128)} copy(f32[1024,3,128]{0,2,1:T(8,128)S(1)} %convolution_bitcast_fusion) | data formatting | bytes 3145728 | tf_op jit(solution)/shard_map/rd,jrc->djc/dot_general | solution.py:167
  70.2 1.4 convolution_bitcast_fusion.1
  71.7 1.0 copy.80
  72.6 3.6 %all-to-all-start.1 = ((f32[16,3,2,8,128]{4,2,3,1,0:T(2,128)}), f32[16,3,2,8,128]{4,2,3,1,0:T(2,128)S(1)}, u32[]{:S(2)}, u32[]{:S(2)}) async-start(f32[16,3,2,8,128]{4,2,3,1,0:T(2,128)} %bitcast.66), calls=%async_computation.1 | async-start | bytes 786432 | tf_op jit(solution)/shard_map/all_to_all | solution.py:159
  76.2 0.6 dynamic-slice
  77.4 11.9 %all-to-all-done.1 = f32[16,3,2,8,128]{4,2,3,1,0:T(2,128)S(1)} async-done(((f32[16,3,2,8,128]{4,2,3,1,0:T(2,128)}), f32[16,3,2,8,128]{4,2,3,1,0:T(2,128)S(1)}, u32[]{:S(2)}, u32[]{:S(2)}) %all-to-all-start.1) | async-done | bytes 393248 | tf_op jit(solution)/shard_map/all_to_all | solution.py:159
  89.4 0.8 copy.64
  90.2 0.8 copy.66
  90.9 0.8 copy.67
  91.7 69.3 %all-reduce.3.cloned.1.call-done = f32[1024,3,128]{2,1,0:T(4,128)} async-done(((f32[1024,3,128]{2,1,0:T(4,128)}), f32[1024,3,128]{2,1,0:T(4,128)}) %all-reduce.3.cloned.1.call-update) | async-done | bytes 1572880
  160.9 0.9 constant_dynamic-slice_fusion
  161.9 0.6 copy.65
  (16 shorter events, 0.4 us)
Async XLA Ops:
  8.0 17.6 %copy-start = (bf16[1024,3,128]{2,0,1:T(8,128)(2,1)S(1)}, bf16[1024,3,128]{2,0,1:T(8,128)(2,1)}, u32[]{:S(2)}) copy-start(bf16[1024,3,128]{2,0,1:T(8,128)(2,1)} %param.11) | copy-start | bytes 2359300
  8.0 152.9 %all-reduce.3.cloned.1.call-start = ((), (), s32[]{:S(2)}) async-start(), calls=%async_computation.5 | async-start | bytes 4194304
  70.1 1.6 copy-start.1
  70.1 6.1 %copy-start.2 = (u32[128]{0:T(128)S(1)}, u32[128]{0:T(128)}, u32[]{:S(2)}) copy-start(u32[128]{0:T(128)} %constant.17) | copy-start | bytes 1540
  70.1 92.4 %reduce-scatter.2.cloned.1.call-start = ((), (), s32[]{:S(2)}) async-start(), calls=%async_computation.4 | async-start | bytes 1179648 | tf_op jit(solution)/shard_map/reduce_scatter | solution.py:165
  72.6 16.7 %all-to-all-start.1 = ((f32[16,3,2,8,128]{4,2,3,1,0:T(2,128)}), f32[16,3,2,8,128]{4,2,3,1,0:T(2,128)S(1)}, u32[]{:S(2)}, u32[]{:S(2)}) async-start(f32[16,3,2,8,128]{4,2,3,1,0:T(2,128)} %bitcast.66), calls=%async_computation.1 | async-start | bytes 786432 | tf_op jit(solution)/shard_map/all_to_all | solution.py:159
Sparse Core Ops, SparseCore 0:
  70.2 90.6 all-reduce.2
Sparse Core Ops, SparseCore 1:
  73.6 27.9 reduce-scatter.1

commit v2 on v1

v2 whole, which is shorter than its diff:
```python
import functools

import jax
import jax.numpy as jnp
import numpy as np
from jax import lax
from jax.experimental import pallas as pl
from jax.experimental.pallas import tpu as pltpu
from jax.sharding import PartitionSpec as P

OUTER = 32
INNER = 128
LENGTH = OUTER * INNER
CH = 8
ROWS = OUTER * CH
BF16 = jnp.bfloat16
F32 = jnp.float32


def split_const(matrix):
    high = matrix.astype(np.float32).astype(BF16)
    low = (matrix - high.astype(np.float64)).astype(np.float32).astype(BF16)
    return high, low


def tables():
    outer = np.arange(OUTER)
    inner = np.arange(INNER)
    shifted = outer + 0.25
    theta = 2 * np.pi * np.outer(shifted, outer) / OUTER
    eye = np.eye(CH)
    forward = np.concatenate([np.kron(np.cos(theta), eye), np.kron(-np.sin(theta), eye)], axis=0)
    backward = np.concatenate([np.kron(np.cos(theta.T), eye), np.kron(-np.sin(theta.T), eye)], axis=1) / LENGTH
    psi = 2 * np.pi * (np.outer(inner, inner) % INNER) / INNER
    cos, sin = np.cos(psi), np.sin(psi)
    dft = np.block([[cos, -sin], [sin, cos]])
    idft = np.block([[cos, sin], [-sin, cos]])
    phi = np.repeat(2 * np.pi * np.outer(shifted, inner) / LENGTH, CH, axis=0)
    fwd = np.concatenate(split_const(forward), axis=1)
    bwd = np.concatenate(split_const(backward), axis=1)
    dft2 = np.concatenate(split_const(dft), axis=0)
    idft2 = np.concatenate(split_const(idft), axis=0)
    twiddle = np.stack([np.cos(phi), np.sin(phi)]).astype(np.float32)
    return fwd, bwd, dft2, idft2, twiddle


def halves(value):
    high = value.astype(BF16)
    low = (value - high.astype(F32)).astype(BF16)
    return high, low


def product(left, right):
    return jnp.dot(left, right, preferred_element_type=F32)


def thrice(table, axis):
    high, low = jnp.split(table, 2, axis=axis)
    return jnp.concatenate([high, low, high], axis=axis)


def to_spectra(signals, fwd_ref, dft_ref, cos, sin):
    high, low = halves(jnp.concatenate(signals, axis=1))
    stage = product(thrice(fwd_ref[...], 1), jnp.concatenate([high, high, low], axis=0))
    rows = []
    for n in range(len(signals)):
        real = stage[:ROWS, n * INNER : (n + 1) * INNER]
        imag = stage[ROWS:, n * INNER : (n + 1) * INNER]
        rows.append(jnp.concatenate([real * cos + imag * sin, imag * cos - real * sin], axis=1))
    high, low = halves(jnp.concatenate(rows, axis=0))
    out = product(jnp.concatenate([high, high, low], axis=1), thrice(dft_ref[...], 0))
    return [
        (out[n * ROWS : (n + 1) * ROWS, :INNER], out[n * ROWS : (n + 1) * ROWS, INNER:])
        for n in range(len(signals))
    ]


def to_signals(spectra, bwd_ref, idft_ref, cos, sin):
    stacked = jnp.concatenate([jnp.concatenate(pair, axis=1) for pair in spectra], axis=0)
    high, low = halves(stacked)
    out = product(jnp.concatenate([high, high, low], axis=1), thrice(idft_ref[...], 0))
    columns = []
    for n in range(len(spectra)):
        real = out[n * ROWS : (n + 1) * ROWS, :INNER]
        imag = out[n * ROWS : (n + 1) * ROWS, INNER:]
        columns.append(jnp.concatenate([real * cos - imag * sin, imag * cos + real * sin], axis=0))
    high, low = halves(jnp.concatenate(columns, axis=1))
    signals = product(thrice(bwd_ref[...], 1), jnp.concatenate([high, high, low], axis=0))
    return [signals[:, n * INNER : (n + 1) * INNER] for n in range(len(spectra))]


def times(first, second):
    return first[0] * second[0] - first[1] * second[1], first[0] * second[1] + first[1] * second[0]


def times_conj(first, second):
    return first[0] * second[0] + first[1] * second[1], first[1] * second[0] - first[0] * second[1]


SEQ = 16
CHAN = 8
RING = 4
MESH = pl.DeviceIdType.MESH


def to_blocks(array):
    return [array[n * INNER : (n + 1) * INNER, :].T.reshape(SEQ, CH, INNER) for n in range(2)]


def chain_kernel(
    tok_hbm, w_hbm, one_hbm, two_hbm, grad_hbm, fwd_hbm, bwd_hbm, dft_hbm, idft_hbm, twiddle_hbm,
    sig_out, token_out, proj_out,
    tok, weights, local, fwd, bwd, dft, idft, twiddle, tok_t,
    send_a, recv_a, send_b, recv_b, send_g, recv_g, send_f, send_t, send_p,
    load_sem, tok_send, tok_recv, a_send, a_recv, b_send, b_recv, g_send, g_recv, f_send, f_recv,
    t_send, t_recv, p_send, p_recv, own_sem,
):
    me = lax.axis_index("seq")
    chan = lax.axis_index("chan")
    core = lax.rem(chan, 2)
    chip = lax.div(chan, 2)
    plane = lax.div(me, RING)
    row = lax.rem(me, RING)

    loads = [
        pltpu.make_async_copy(source, target, load_sem.at[n])
        for n, (source, target) in enumerate(
            [
                (tok_hbm, tok.at[chan]),
                (one_hbm, local.at[0]),
                (two_hbm, local.at[1]),
                (grad_hbm, local.at[2]),
                (w_hbm, weights),
                (fwd_hbm, fwd),
                (dft_hbm, dft),
                (twiddle_hbm, twiddle),
                (bwd_hbm, bwd),
                (idft_hbm, idft),
            ]
        )
    ]
    for load in loads:
        load.start()

    barrier = pltpu.get_barrier_semaphore()

    def greet_seq(k, carry):
        pl.semaphore_signal(
            barrier, inc=1, device_id=(lax.rem(me + k, SEQ), chan), device_id_type=MESH
        )
        return carry

    def greet_chan(k, carry):
        pl.semaphore_signal(
            barrier, inc=1, device_id=(me, lax.rem(chan + k, CHAN)), device_id_type=MESH
        )
        return carry

    lax.fori_loop(1, CHAN, greet_chan, 0)
    lax.fori_loop(1, SEQ, greet_seq, 0)
    pl.semaphore_wait(barrier, SEQ + CHAN - 2)

    def token_copy(source, slot, send, target):
        return pltpu.make_async_remote_copy(
            src_ref=source,
            dst_ref=tok.at[slot],
            send_sem=tok_send.at[send],
            recv_sem=tok_recv.at[slot],
            device_id=(me, target),
            device_id_type=MESH,
        )

    def across(k):
        return lax.rem(chip + k, RING) * 2 + core

    sibling = chip * 2 + (1 - core)
    own_sends = [token_copy(tok_hbm, chan, k, across(k)) for k in (2, 1, 3)]
    own_sends.append(token_copy(tok_hbm, chan, 0, sibling))
    for copy in own_sends:
        copy.start()

    def exchange(send, recv, send_sem, recv_sem):
        def copy(target, slot):
            return pltpu.make_async_remote_copy(
                src_ref=send.at[target],
                dst_ref=recv.at[slot],
                send_sem=send_sem.at[target],
                recv_sem=recv_sem.at[slot],
                device_id=(target, chan),
                device_id_type=MESH,
            )

        def start(k, carry):
            copy(lax.rem(me + k, SEQ), me).start()
            return carry

        def wait_recv(k, carry):
            source = lax.rem(me + SEQ - k, SEQ)
            copy(source, source).wait_recv()
            return carry

        def wait_send(k, carry):
            target = lax.rem(me + k, SEQ)
            copy(target, me).wait_send()
            return carry

        return tuple(
            functools.partial(lax.fori_loop, 1, SEQ, step, 0) for step in (start, wait_recv, wait_send)
        )

    a_start, a_arrive, a_leave = exchange(send_a, recv_a, a_send, a_recv)
    b_start, b_arrive, b_leave = exchange(send_b, recv_b, b_send, b_recv)
    g_start, g_arrive, g_leave = exchange(send_g, recv_g, g_send, g_recv)
    f_start, f_arrive, f_leave = exchange(send_f, sig_out, f_send, f_recv)

    for n in range(3):
        loads[1 + n].wait()
    for n in range(3):
        for half, block in enumerate(to_blocks(local[n])):
            send_a[:, n, half * CH : (half + 1) * CH, :] = block
    a_start()
    recv_a[me] = send_a[me]

    loads[0].wait()
    loads[4].wait()
    relays = []
    for n, k in enumerate((1, 3, 2)):
        slot = lax.rem(chip + RING - k, RING) * 2 + core
        token_copy(tok.at[slot], slot, 4 + n, sibling).wait_recv()
        relay = token_copy(tok.at[slot], slot, 4 + n, sibling)
        relay.start()
        relays.append(relay)
    for k in range(RING):
        slot = lax.rem(chip + k, RING) * 2 + (1 - core)
        token_copy(tok.at[slot], slot, 0, sibling).wait_recv()

    full = jnp.concatenate([tok[k] for k in range(CHAN)], axis=1)
    w_flat = jnp.concatenate([weights[j] for j in range(3)], axis=1)
    projected = product(full, w_flat)
    for n in range(3):
        for half, block in enumerate(to_blocks(projected[:, n * INNER : (n + 1) * INNER])):
            send_b[:, n, half * CH : (half + 1) * CH, :] = block
    b_start()
    recv_b[me] = send_b[me]

    for k in range(CHAN):
        tok_t[k * INNER : (k + 1) * INNER, :] = tok[k].T
    for n in range(5, 10):
        loads[n].wait()
    a_arrive()
    cos, sin = twiddle[0], twiddle[1]
    filter_one, filter_two, out_grad = [recv_a[:, n].reshape(ROWS, INNER) for n in range(3)]
    spec_one, spec_two = to_spectra([filter_one, filter_two], fwd, dft, cos, sin)

    b_arrive()
    values, gate_one, gate_two = [recv_b[:, n].reshape(ROWS, INNER) for n in range(3)]
    grad_two = out_grad * gate_two
    spec_values, spec_grad_two = to_spectra([values, grad_two], fwd, dft, cos, sin)
    mixed_one, grad_inner = to_signals(
        [times(spec_one, spec_values), times_conj(spec_grad_two, spec_two)], bwd, idft, cos, sin
    )
    inner = gate_one * mixed_one
    grad_one = grad_inner * gate_one
    spec_inner, spec_grad_one = to_spectra([inner, grad_one], fwd, dft, cos, sin)
    mixed_two, grad_values = to_signals(
        [times(spec_two, spec_inner), times_conj(spec_grad_one, spec_one)], bwd, idft, cos, sin
    )
    for n, grad in enumerate((grad_values, grad_inner * mixed_one, out_grad * mixed_two)):
        send_g[:, n] = grad.astype(BF16).reshape(SEQ, 2 * CH, INNER)
    g_start()
    recv_g[me] = send_g[me]
    filter_two_grad, filter_one_grad = to_signals(
        [times_conj(spec_grad_two, spec_inner), times_conj(spec_grad_one, spec_values)], bwd, idft, cos, sin
    )
    for n, signal in enumerate((gate_two * mixed_two, filter_one_grad, filter_two_grad)):
        send_f[:, n] = signal.reshape(SEQ, 2 * CH, INNER)
    f_start()
    own_f = pltpu.make_async_copy(send_f.at[me], sig_out.at[me], own_sem.at[0])
    own_f.start()

    g_arrive()
    columns = []
    for n in range(3):
        arrived = recv_g[:, n].astype(F32)
        columns.append(
            jnp.concatenate(
                [
                    arrived[:, half * CH : (half + 1) * CH, :].reshape(INNER, INNER).T.astype(BF16)
                    for half in range(2)
                ],
                axis=0,
            )
        )
    grads = jnp.concatenate(columns, axis=1)

    def proj_copy(target, slot):
        return pltpu.make_async_remote_copy(
            src_ref=send_p.at[target],
            dst_ref=proj_out.at[slot],
            send_sem=p_send.at[target],
            recv_sem=p_recv.at[slot],
            device_id=(target, chan),
            device_id_type=MESH,
        )

    def term_copy(target, slot):
        return pltpu.make_async_remote_copy(
            src_ref=send_t.at[target],
            dst_ref=token_out.at[slot],
            send_sem=t_send.at[target],
            recv_sem=t_recv.at[slot],
            device_id=(me, target),
            device_id_type=MESH,
        )

    depth = 1024 // SEQ
    for step in (2, 1, 3, 4):
        base = lax.rem(plane + step, RING) * RING
        slab = product(tok_t[pl.ds(pl.multiple_of(base * depth, 256), 256), :], grads).astype(BF16)
        for n in range(RING):
            for j in range(3):
                send_p[base + n, j] = slab[n * depth : (n + 1) * depth, j * INNER : (j + 1) * INNER]
        for n in (2, 1, 3, 0):
            if step < 4 or n > 0:
                proj_copy(base + lax.rem(row + n, RING), me).start()
        base = lax.rem(chip + step, RING) * 2
        columns = pl.ds(pl.multiple_of(base * INNER, 256), 256)
        w_rows = jnp.concatenate([weights[j, columns, :] for j in range(3)], axis=1)
        terms = lax.dot_general(grads, w_rows, (((1,), (1,)), ((), ())), preferred_element_type=F32)
        for n in range(2):
            send_t[base + n] = terms[:, n * INNER : (n + 1) * INNER].astype(BF16)
        if step < 4:
            term_copy(base + core, chan).start()
        term_copy(base + (1 - core), chan).start()
    own_p = pltpu.make_async_copy(send_p.at[me], proj_out.at[me], own_sem.at[1])
    own_p.start()
    own_t = pltpu.make_async_copy(send_t.at[chan], token_out.at[chan], own_sem.at[2])
    own_t.start()

    for copy in own_sends + relays:
        copy.wait_send()
    a_leave()
    b_leave()
    g_leave()
    f_arrive()
    f_leave()

    def finish_term(k, carry):
        source = lax.rem(chan + CHAN - k, CHAN)
        term_copy(source, source).wait_recv()
        target = lax.rem(chan + k, CHAN)
        term_copy(target, chan).wait_send()
        return carry

    def finish_proj(k, carry):
        source = lax.rem(me + SEQ - k, SEQ)
        proj_copy(source, source).wait_recv()
        target = lax.rem(me + k, SEQ)
        proj_copy(target, me).wait_send()
        return carry

    lax.fori_loop(1, CHAN, finish_term, 0)
    lax.fori_loop(1, SEQ, finish_proj, 0)
    own_f.wait()
    own_p.wait()
    own_t.wait()


def finish_kernel(sig_ref, token_ref, proj_ref, output_ref, token_grad_ref, proj_grad_ref, one_ref, two_ref):
    for n, ref in enumerate((output_ref, one_ref, two_ref)):
        for half in range(2):
            block = sig_ref[:, n, half * CH : (half + 1) * CH, :].reshape(INNER, INNER)
            ref[half * INNER : (half + 1) * INNER, :] = block.T
    token_grad_ref[...] = sum(token_ref[k].astype(F32) for k in range(CHAN))
    proj_grad_ref[...] = sum(proj_ref[k].astype(F32) for k in range(SEQ))


def shards(tokens, in_proj, filter_one, filter_two, out_grad):
    rows, width = tokens.shape
    depth = in_proj.shape[0]
    anywhere = pl.BlockSpec(memory_space=pl.ANY)
    dma = pltpu.SemaphoreType.DMA
    block = (SEQ, 3, 2 * CH, INNER)
    fwd, bwd, dft, idft, twiddle = tables()
    arrived = pl.pallas_call(
        chain_kernel,
        out_shape=(
            jax.ShapeDtypeStruct(block, F32),
            jax.ShapeDtypeStruct((CHAN, rows, width), BF16),
            jax.ShapeDtypeStruct((SEQ, 3, depth // SEQ, width), BF16),
        ),
        in_specs=[anywhere] * 10,
        out_specs=(anywhere,) * 3,
        scratch_shapes=[
            pltpu.VMEM((CHAN, rows, width), BF16),
            pltpu.VMEM((3, depth, width), BF16),
            pltpu.VMEM((3, rows, width), F32),
            pltpu.VMEM(fwd.shape, BF16),
            pltpu.VMEM(bwd.shape, BF16),
            pltpu.VMEM(dft.shape, BF16),
            pltpu.VMEM(idft.shape, BF16),
            pltpu.VMEM(twiddle.shape, F32),
            pltpu.VMEM((depth, rows), BF16),
            pltpu.VMEM(block, F32),
            pltpu.VMEM(block, F32),
            pltpu.VMEM(block, F32),
            pltpu.VMEM(block, F32),
            pltpu.VMEM(block, BF16),
            pltpu.VMEM(block, BF16),
            pltpu.VMEM(block, F32),
            pltpu.VMEM((CHAN, rows, width), BF16),
            pltpu.VMEM((SEQ, 3, depth // SEQ, width), BF16),
            dma((10,)),
            dma((8,)),
            dma((8,)),
        ]
        + [dma((SEQ,))] * 8
        + [dma((CHAN,)), dma((CHAN,)), dma((SEQ,)), dma((SEQ,)), dma((3,))],
        compiler_params=pltpu.CompilerParams(collective_id=0, has_side_effects=True),
        name="chain",
    )(
        tokens,
        in_proj.transpose(1, 0, 2),
        filter_one,
        filter_two,
        out_grad,
        *[jnp.asarray(t) for t in (fwd, bwd, dft, idft, twiddle)],
    )
    vmem = pl.BlockSpec(memory_space=pltpu.VMEM)
    flat = jax.ShapeDtypeStruct((rows, width), F32)
    output, token_grad, proj_grad, one, two = pl.pallas_call(
        finish_kernel,
        out_shape=(flat, flat, jax.ShapeDtypeStruct((3, depth // SEQ, width), F32), flat, flat),
        in_specs=[vmem] * 3,
        out_specs=(vmem,) * 5,
        name="finish",
    )(*arrived)
    return output, token_grad, proj_grad.transpose(1, 0, 2), one, two


def solution(mesh):
    in_specs = (
        P("seq", "chan"),
        P(None, None, "chan"),
        P("seq", "chan"),
        P("seq", "chan"),
        P("seq", "chan"),
    )
    out_specs = (
        P("seq", "chan"),
        P("seq", "chan"),
        P("seq", None, "chan"),
        P("seq", "chan"),
        P("seq", "chan"),
    )
    return jax.shard_map(shards, mesh=mesh, in_specs=in_specs, out_specs=out_specs, check_vma=False)
```

time: 171 us -> 49.6 us (0.29)
  waiting for transfers between devices: 81.2 us -> 0 us
  blocking collectives: 46.2 us -> 0 us
  Pallas kernels: 7.75 us -> 48.8 us
  between operations: 16.3 us -> 0.64 us
  local copies, waits for them, and re-layouts: 12.6 us -> 0 us
  starting transfers between devices: 3.63 us -> 0 us
  matrix products: 2.23 us -> 0 us
    unnamed x3 -> x0, waiting for transfers between devices: 69.3 us -> none
    pallas_call x1 -> x2, Pallas kernels: 7.75 us -> 48.8 us  [the longest x1 46.5 us: shards(): pl.pallas_call(chain_kernel, out_shape=(jax.ShapeDtypeStruct(block, F32),...]
    all_to_all x2 -> x0, blocking collectives: 31.8 us -> none  [the longest x1 21.6 us: shards(): arrived = lax.all_to_all(blocks.transpose(0, 1, 3, 2, 4), 'seq', 0, 0)]
    all_gather x1 -> x0, blocking collectives: 14.5 us -> none  [shards(): full_tokens = lax.all_gather(tokens, 'chan', axis=1, tiled=True)]
    all_to_all x1 -> x0, waiting for transfers between devices: 11.9 us -> none  [back(): home = lax.all_to_all(parted, 'seq', 0, 0)]
    unnamed x17 -> x0, local copies, waits for them, and re-layouts: 7.54 us -> none
    all_to_all x1 -> x0, starting transfers between devices: 3.55 us -> none  [back(): home = lax.all_to_all(parted, 'seq', 0, 0)]
    dot_general x3 -> x0, matrix products: 2.23 us -> none  [the longest x1 1.44 us: shards(): jnp.einsum('jrc,djc->rd', grads, in_proj, preferred_element_type=F32)]
  transfers between devices with their start and end apart: 3 -> 0, of which waited for: 2 -> 0; matrix products, arithmetic and copies ran while one was open for 4% -> 0% of each run, Pallas kernels for 0% -> 0%
where the time goes in v2:
time: 49.6 us; the launch traced here: 49.5 us
  Pallas kernels  48.8 us (98%)
  between operations  0.64 us (1%)
    pallas_call x1, Pallas kernels, shards(): pl.pallas_call(chain_kernel, out_shape=(jax.ShapeDtypeStruct(block, F32),...  46.5 us
    pallas_call x1, Pallas kernels, shards(): pl.pallas_call(finish_kernel, out_shape=(flat, flat, jax.ShapeDtypeStruct...  2.33 us

profile of v2, /device:TPU:1, one launch (start us, length us, event | category | flops | bytes accessed | tf_op | source)
XLA Modules:
  0.0 49.5 jit_solution(2973296014910992653)
XLA Ops:
  0.6 46.5 %chain.1 = (f32[16,3,16,128]{3,2,1,0:T(8,128)}, bf16[8,256,128]{2,1,0:T(8,128)(2,1)}, bf16[16,3,64,128]{3,2,1,0:T(8,128)(2,1)}) custom-call(bf16[256,128]{1,0:T(8,128)(2,1)} %tok_hbm.1, bf16[3,1024,128]{2,1,0:T(8,128)(2,1)} %bitcast.2, f32[256,128]{1,0:T(8,128)} %one_hbm.1, f32[256,128]{1,0:T(8,128)} %two_hbm.1, f32[256,128]{1,0:T(8,128)} %grad_hbm.1, ...), custom_call_target="tpu_custom_call" | custom-call | tf_op jit(solution)/shard_map/chain/pallas_call | solution.py:385
  47.1 2.3 %finish.1 = (f32[256,128]{1,0:T(8,128)}, f32[256,128]{1,0:T(8,128)}, f32[3,64,128]{2,1,0:T(8,128)}, f32[256,128]{1,0:T(8,128)}, f32[256,128]{1,0:T(8,128)}) custom-call(f32[16,3,16,128]{3,2,1,0:T(8,128)} %get-tuple-element.13.sig_ref, bf16[8,256,128]{2,1,0:T(8,128)(2,1)} %get-tuple-element.14.token_ref, bf16[16,3,64,128]{3,2,1,0:T(8,128)(2,1)} %get-tuple-element.15.proj_ref), custom_call_target="tpu_custom_call" | custom-call | tf_op jit(solution)/shard_map/finish/pallas_call | solution.py:431

commit v3 on v2

--- a/solution.py
+++ b/solution.py
@@ -111,9 +111,10 @@
     tok_hbm, w_hbm, one_hbm, two_hbm, grad_hbm, fwd_hbm, bwd_hbm, dft_hbm, idft_hbm, twiddle_hbm,
     sig_out, token_out, proj_out,
     tok, weights, local, fwd, bwd, dft, idft, twiddle, tok_t,
-    send_a, recv_a, send_b, recv_b, send_g, recv_g, send_f, send_t, send_p,
+    send_a, recv_a, send_b, recv_b, send_g, recv_g, send_f, send_t,
+    slabs, send_y, recv_y, send_z, recv_z, send_q,
     load_sem, tok_send, tok_recv, a_send, a_recv, b_send, b_recv, g_send, g_recv, f_send, f_recv,
-    t_send, t_recv, p_send, p_recv, own_sem,
+    t_send, t_recv, y_send, y_recv, z_send, z_recv, q_send, q_recv, own_sem,
 ):
     me = lax.axis_index("seq")
     chan = lax.axis_index("chan")
@@ -158,6 +159,11 @@
 
     lax.fori_loop(1, CHAN, greet_chan, 0)
     lax.fori_loop(1, SEQ, greet_seq, 0)
+    for n in range(3):
+        loads[1 + n].wait()
+    for n in range(3):
+        for half, block in enumerate(to_blocks(local[n])):
+            send_a[:, n, half * CH : (half + 1) * CH, :] = block
     pl.semaphore_wait(barrier, SEQ + CHAN - 2)
 
     def token_copy(source, slot, send, target):
@@ -213,11 +219,6 @@
     g_start, g_arrive, g_leave = exchange(send_g, recv_g, g_send, g_recv)
     f_start, f_arrive, f_leave = exchange(send_f, sig_out, f_send, f_recv)
 
-    for n in range(3):
-        loads[1 + n].wait()
-    for n in range(3):
-        for half, block in enumerate(to_blocks(local[n])):
-            send_a[:, n, half * CH : (half + 1) * CH, :] = block
     a_start()
     recv_a[me] = send_a[me]
 
@@ -273,7 +274,7 @@
         [times_conj(spec_grad_two, spec_inner), times_conj(spec_grad_one, spec_values)], bwd, idft, cos, sin
     )
     for n, signal in enumerate((gate_two * mixed_two, filter_one_grad, filter_two_grad)):
-        send_f[:, n] = signal.reshape(SEQ, 2 * CH, INNER)
+        send_f[:, n] = signal.astype(BF16).reshape(SEQ, 2 * CH, INNER)
     f_start()
     own_f = pltpu.make_async_copy(send_f.at[me], sig_out.at[me], own_sem.at[0])
     own_f.start()
@@ -293,12 +294,32 @@
         )
     grads = jnp.concatenate(columns, axis=1)
 
-    def proj_copy(target, slot):
+    def y_copy(step, target, slot):
         return pltpu.make_async_remote_copy(
-            src_ref=send_p.at[target],
-            dst_ref=proj_out.at[slot],
-            send_sem=p_send.at[target],
-            recv_sem=p_recv.at[slot],
+            src_ref=send_y.at[step, target],
+            dst_ref=recv_y.at[step, slot],
+            send_sem=y_send.at[step * RING + target],
+            recv_sem=y_recv.at[step * RING + slot],
+            device_id=(plane * RING + target, chan),
+            device_id_type=MESH,
+        )
+
+    def z_copy(step, target, slot):
+        return pltpu.make_async_remote_copy(
+            src_ref=send_z.at[step],
+            dst_ref=recv_z.at[slot],
+            send_sem=z_send.at[step],
+            recv_sem=z_recv.at[slot],
+            device_id=(target * RING + row, chan),
+            device_id_type=MESH,
+        )
+
+    def q_copy(side, step, target, slot):
+        return pltpu.make_async_remote_copy(
+            src_ref=send_q.at[side, step],
+            dst_ref=proj_out.at[side, slot],
+            send_sem=q_send.at[side * RING + step],
+            recv_sem=q_recv.at[side * RING + slot],
             device_id=(target, chan),
             device_id_type=MESH,
         )
@@ -314,15 +335,26 @@
         )
 
     depth = 1024 // SEQ
-    for step in (2, 1, 3, 4):
-        base = lax.rem(plane + step, RING) * RING
-        slab = product(tok_t[pl.ds(pl.multiple_of(base * depth, 256), 256), :], grads).astype(BF16)
+    part = depth // 2
+    first_sends = []
+    for i, step in enumerate((2, 1, 3, 4)):
+        target_plane = lax.rem(plane + step, RING)
+        slab = product(
+            tok_t[pl.ds(pl.multiple_of(target_plane * (RING * depth), 256), RING * depth), :], grads
+        )
+        slabs[i] = slab
+        rounded = slab.astype(BF16)
         for n in range(RING):
             for j in range(3):
-                send_p[base + n, j] = slab[n * depth : (n + 1) * depth, j * INNER : (j + 1) * INNER]
-        for n in (2, 1, 3, 0):
-            if step < 4 or n > 0:
-                proj_copy(base + lax.rem(row + n, RING), me).start()
+                cut = rounded[n * depth : (n + 1) * depth, j * INNER : (j + 1) * INNER]
+                send_y[i, n, j] = cut[:part]
+                send_z[i, n, j] = cut[part:]
+        for n in (2, 1, 3):
+            first_sends.append(y_copy(i, lax.rem(row + n, RING), row))
+            first_sends[-1].start()
+        if step < 4:
+            first_sends.append(z_copy(i, target_plane, plane))
+            first_sends[-1].start()
         base = lax.rem(chip + step, RING) * 2
         columns = pl.ds(pl.multiple_of(base * INNER, 256), 256)
         w_rows = jnp.concatenate([weights[j, columns, :] for j in range(3)], axis=1)
@@ -332,10 +364,45 @@
         if step < 4:
             term_copy(base + core, chan).start()
         term_copy(base + (1 - core), chan).start()
-    own_p = pltpu.make_async_copy(send_p.at[me], proj_out.at[me], own_sem.at[1])
-    own_p.start()
     own_t = pltpu.make_async_copy(send_t.at[chan], token_out.at[chan], own_sem.at[2])
     own_t.start()
+
+    rows_y = [lax.rem(row + k, RING) for k in range(RING)]
+    planes_z = [lax.rem(plane + k, RING) for k in range(RING)]
+    second_sends = []
+
+    def sum_y(i):
+        for source in rows_y[1:]:
+            y_copy(i, source, source).wait_recv()
+        mine = slabs[i, pl.ds(pl.multiple_of(row * depth, depth), part), :]
+        for j in range(3):
+            total = mine[:, j * INNER : (j + 1) * INNER]
+            for source in rows_y[1:]:
+                total += recv_y[i, source, j].astype(F32)
+            send_q[0, i, j] = total.astype(BF16)
+
+    for i, step in enumerate((2, 1, 3)):
+        sum_y(i)
+        second_sends.append(q_copy(0, i, planes_z[step] * RING + row, plane))
+        second_sends[-1].start()
+    for source in planes_z[1:]:
+        z_copy(0, source, source).wait_recv()
+    for n in (2, 1, 3, 0):
+        target = rows_y[n]
+        mine = slabs[3, pl.ds(pl.multiple_of(target * depth + part, part), part), :]
+        for j in range(3):
+            total = mine[:, j * INNER : (j + 1) * INNER]
+            for source in planes_z[1:]:
+                total += recv_z[source, target, j].astype(F32)
+            send_q[1, n, j] = total.astype(BF16)
+        if n > 0:
+            second_sends.append(q_copy(1, n, plane * RING + target, row))
+            second_sends[-1].start()
+    sum_y(3)
+    own_y = pltpu.make_async_copy(send_q.at[0, 3], proj_out.at[0, plane], own_sem.at[1])
+    own_y.start()
+    own_z = pltpu.make_async_copy(send_q.at[1, 0], proj_out.at[1, row], own_sem.at[3])
+    own_z.start()
 
     for copy in own_sends + relays:
         copy.wait_send()
@@ -352,27 +419,29 @@
         term_copy(target, chan).wait_send()
         return carry
 
-    def finish_proj(k, carry):
-        source = lax.rem(me + SEQ - k, SEQ)
-        proj_copy(source, source).wait_recv()
-        target = lax.rem(me + k, SEQ)
-        proj_copy(target, me).wait_send()
-        return carry
-
     lax.fori_loop(1, CHAN, finish_term, 0)
-    lax.fori_loop(1, SEQ, finish_proj, 0)
+    for k in range(1, RING):
+        q_copy(0, 0, me, planes_z[k]).wait_recv()
+        q_copy(1, 0, me, rows_y[k]).wait_recv()
+    for copy in first_sends + second_sends:
+        copy.wait_send()
     own_f.wait()
-    own_p.wait()
+    own_y.wait()
+    own_z.wait()
     own_t.wait()
 
 
 def finish_kernel(sig_ref, token_ref, proj_ref, output_ref, token_grad_ref, proj_grad_ref, one_ref, two_ref):
     for n, ref in enumerate((output_ref, one_ref, two_ref)):
         for half in range(2):
-            block = sig_ref[:, n, half * CH : (half + 1) * CH, :].reshape(INNER, INNER)
+            block = sig_ref[:, n, half * CH : (half + 1) * CH, :].astype(F32).reshape(INNER, INNER)
             ref[half * INNER : (half + 1) * INNER, :] = block.T
     token_grad_ref[...] = sum(token_ref[k].astype(F32) for k in range(CHAN))
-    proj_grad_ref[...] = sum(proj_ref[k].astype(F32) for k in range(SEQ))
+    part = proj_ref.shape[3]
+    for side in range(2):
+        proj_grad_ref[:, side * part : (side + 1) * part, :] = sum(
+            proj_ref[side, k].astype(F32) for k in range(RING)
+        )
 
 
 def shards(tokens, in_proj, filter_one, filter_two, out_grad):
@@ -385,9 +454,9 @@
     arrived = pl.pallas_call(
         chain_kernel,
         out_shape=(
-            jax.ShapeDtypeStruct(block, F32),
+            jax.ShapeDtypeStruct(block, BF16),
             jax.ShapeDtypeStruct((CHAN, rows, width), BF16),
-            jax.ShapeDtypeStruct((SEQ, 3, depth // SEQ, width), BF16),
+            jax.ShapeDtypeStruct((2, RING, 3, depth // SEQ // 2, width), BF16),
         ),
         in_specs=[anywhere] * 10,
         out_specs=(anywhere,) * 3,
@@ -407,15 +476,24 @@
             pltpu.VMEM(block, F32),
             pltpu.VMEM(block, BF16),
             pltpu.VMEM(block, BF16),
-            pltpu.VMEM(block, F32),
+            pltpu.VMEM(block, BF16),
             pltpu.VMEM((CHAN, rows, width), BF16),
-            pltpu.VMEM((SEQ, 3, depth // SEQ, width), BF16),
+            pltpu.VMEM((RING, depth // RING, 3 * width), F32),
+            pltpu.VMEM((RING, RING, 3, depth // SEQ // 2, width), BF16),
+            pltpu.VMEM((RING, RING, 3, depth // SEQ // 2, width), BF16),
+            pltpu.VMEM((RING, RING, 3, depth // SEQ // 2, width), BF16),
+            pltpu.VMEM((RING, RING, 3, depth // SEQ // 2, width), BF16),
+            pltpu.VMEM((2, RING, 3, depth // SEQ // 2, width), BF16),
             dma((10,)),
             dma((8,)),
             dma((8,)),
         ]
         + [dma((SEQ,))] * 8
-        + [dma((CHAN,)), dma((CHAN,)), dma((SEQ,)), dma((SEQ,)), dma((3,))],
+        + [dma((CHAN,))] * 2
+        + [dma((SEQ,))] * 2
+        + [dma((RING,))] * 2
+        + [dma((2 * RING,))] * 2
+        + [dma((4,))],
         compiler_params=pltpu.CompilerParams(collective_id=0, has_side_effects=True),
         name="chain",
     )(

time: 49.6 us -> 47.1 us (0.950); the launches traced: 49.5 us -> 46.4 us
  Pallas kernels: 48.8 us -> 45.7 us
    pallas_call x1, Pallas kernels: 46.5 us -> 43.7 us  [shards(): pl.pallas_call(chain_kernel, out_shape=(jax.ShapeDtypeStruct(block, BF16)...]
where the time goes in v3:
time: 47.1 us; the launch traced here: 46.4 us
  Pallas kernels  45.7 us (97%)
  between operations  0.64 us (1%)
    pallas_call x1, Pallas kernels, shards(): pl.pallas_call(chain_kernel, out_shape=(jax.ShapeDtypeStruct(block, BF16)...  43.7 us
    pallas_call x1, Pallas kernels, shards(): pl.pallas_call(finish_kernel, out_shape=(flat, flat, jax.ShapeDtypeStruct...  2.06 us

profile of v3, /device:TPU:1, one launch (start us, length us, event | category | flops | bytes accessed | tf_op | source)
XLA Modules:
  0.0 46.4 jit_solution(14090101429343797162)
XLA Ops:
  0.6 43.7 %chain.1 = (bf16[16,3,16,128]{3,2,1,0:T(8,128)(2,1)}, bf16[8,256,128]{2,1,0:T(8,128)(2,1)}, bf16[2,4,3,32,128]{4,3,2,1,0:T(8,128)(2,1)}) custom-call(bf16[256,128]{1,0:T(8,128)(2,1)} %tok_hbm.1, bf16[3,1024,128]{2,1,0:T(8,128)(2,1)} %bitcast.2, f32[256,128]{1,0:T(8,128)} %one_hbm.1, f32[256,128]{1,0:T(8,128)} %two_hbm.1, f32[256,128]{1,0:T(8,128)} %grad_hbm.1, ...), custom_call_target="tpu_custom_call" | custom-call | tf_op jit(solution)/shard_map/chain/pallas_call | solution.py:454
  44.3 2.1 %finish.1 = (f32[256,128]{1,0:T(8,128)}, f32[256,128]{1,0:T(8,128)}, f32[3,64,128]{2,1,0:T(8,128)}, f32[256,128]{1,0:T(8,128)}, f32[256,128]{1,0:T(8,128)}) custom-call(bf16[16,3,16,128]{3,2,1,0:T(8,128)(2,1)} %get-tuple-element.13.sig_ref, bf16[8,256,128]{2,1,0:T(8,128)(2,1)} %get-tuple-element.14.token_ref, ...), custom_call_target="tpu_custom_call" | custom-call | tf_op jit(solution)/shard_map/finish/pallas_call | solution.py:509

commit v4 on v3

--- a/solution.py
+++ b/solution.py
@@ -100,6 +100,8 @@
 SEQ = 16
 CHAN = 8
 RING = 4
+GRAD_ORDER = (1, 0, 2)
+GRAD_GROUPS = ((0, 1), (1, 2))
 MESH = pl.DeviceIdType.MESH
 
 
@@ -111,9 +113,10 @@
     tok_hbm, w_hbm, one_hbm, two_hbm, grad_hbm, fwd_hbm, bwd_hbm, dft_hbm, idft_hbm, twiddle_hbm,
     sig_out, token_out, proj_out,
     tok, weights, local, fwd, bwd, dft, idft, twiddle, tok_t,
-    send_a, recv_a, send_b, recv_b, send_g, recv_g, send_f, send_t,
+    send_a, recv_a, send_b, recv_b, send_c, recv_c, send_g, recv_g, send_h, recv_h, send_f, send_t,
     slabs, send_y, recv_y, send_z, recv_z, send_q,
-    load_sem, tok_send, tok_recv, a_send, a_recv, b_send, b_recv, g_send, g_recv, f_send, f_recv,
+    load_sem, tok_send, tok_recv, a_send, a_recv, b_send, b_recv, c_send, c_recv, g_send, g_recv,
+    h_send, h_recv, f_send, f_recv,
     t_send, t_recv, y_send, y_recv, z_send, z_recv, q_send, q_recv, own_sem,
 ):
     me = lax.axis_index("seq")
@@ -216,7 +219,9 @@
 
     a_start, a_arrive, a_leave = exchange(send_a, recv_a, a_send, a_recv)
     b_start, b_arrive, b_leave = exchange(send_b, recv_b, b_send, b_recv)
+    c_start, c_arrive, c_leave = exchange(send_c, recv_c, c_send, c_recv)
     g_start, g_arrive, g_leave = exchange(send_g, recv_g, g_send, g_recv)
+    h_start, h_arrive, h_leave = exchange(send_h, recv_h, h_send, h_recv)
     f_start, f_arrive, f_leave = exchange(send_f, sig_out, f_send, f_recv)
 
     a_start()
@@ -236,13 +241,16 @@
         token_copy(tok.at[slot], slot, 0, sibling).wait_recv()
 
     full = jnp.concatenate([tok[k] for k in range(CHAN)], axis=1)
-    w_flat = jnp.concatenate([weights[j] for j in range(3)], axis=1)
-    projected = product(full, w_flat)
-    for n in range(3):
+    projected = product(full, jnp.concatenate([weights[0], weights[2]], axis=1))
+    for n in range(2):
         for half, block in enumerate(to_blocks(projected[:, n * INNER : (n + 1) * INNER])):
             send_b[:, n, half * CH : (half + 1) * CH, :] = block
     b_start()
+    for half, block in enumerate(to_blocks(product(full, weights[1]))):
+        send_c[:, 0, half * CH : (half + 1) * CH, :] = block
+    c_start()
     recv_b[me] = send_b[me]
+    recv_c[me] = send_c[me]
 
     for k in range(CHAN):
         tok_t[k * INNER : (k + 1) * INNER, :] = tok[k].T
@@ -254,22 +262,112 @@
     spec_one, spec_two = to_spectra([filter_one, filter_two], fwd, dft, cos, sin)
 
     b_arrive()
-    values, gate_one, gate_two = [recv_b[:, n].reshape(ROWS, INNER) for n in range(3)]
+    values, gate_two = [recv_b[:, n].reshape(ROWS, INNER) for n in range(2)]
     grad_two = out_grad * gate_two
     spec_values, spec_grad_two = to_spectra([values, grad_two], fwd, dft, cos, sin)
     mixed_one, grad_inner = to_signals(
         [times(spec_one, spec_values), times_conj(spec_grad_two, spec_two)], bwd, idft, cos, sin
     )
+    c_arrive()
+    gate_one = recv_c[:, 0].reshape(ROWS, INNER)
+    send_g[:, 0] = (grad_inner * mixed_one).astype(BF16).reshape(SEQ, 2 * CH, INNER)
+    g_start()
+    recv_g[me] = send_g[me]
     inner = gate_one * mixed_one
     grad_one = grad_inner * gate_one
     spec_inner, spec_grad_one = to_spectra([inner, grad_one], fwd, dft, cos, sin)
     mixed_two, grad_values = to_signals(
         [times(spec_two, spec_inner), times_conj(spec_grad_one, spec_one)], bwd, idft, cos, sin
     )
-    for n, grad in enumerate((grad_values, grad_inner * mixed_one, out_grad * mixed_two)):
-        send_g[:, n] = grad.astype(BF16).reshape(SEQ, 2 * CH, INNER)
-    g_start()
-    recv_g[me] = send_g[me]
+    for n, grad in enumerate((grad_values, out_grad * mixed_two)):
+        send_h[:, n] = grad.astype(BF16).reshape(SEQ, 2 * CH, INNER)
+    h_start()
+    recv_h[me] = send_h[me]
+
+    depth = 1024 // SEQ
+    part = depth // 2
+
+    def y_copy(group, step, target, slot):
+        cut = pl.ds(*GRAD_GROUPS[group])
+        base = (group * RING + step) * RING
+        return pltpu.make_async_remote_copy(
+            src_ref=send_y.at[step, target, cut],
+            dst_ref=recv_y.at[step, slot, cut],
+            send_sem=y_send.at[base + target],
+            recv_sem=y_recv.at[base + slot],
+            device_id=(plane * RING + target, chan),
+            device_id_type=MESH,
+        )
+
+    def z_copy(group, step, target, slot):
+        cut = pl.ds(*GRAD_GROUPS[group])
+        return pltpu.make_async_remote_copy(
+            src_ref=send_z.at[step, cut],
+            dst_ref=recv_z.at[slot, cut],
+            send_sem=z_send.at[group * RING + step],
+            recv_sem=z_recv.at[group * RING + slot],
+            device_id=(target * RING + row, chan),
+            device_id_type=MESH,
+        )
+
+    def q_copy(side, step, target, slot):
+        return pltpu.make_async_remote_copy(
+            src_ref=send_q.at[side, step],
+            dst_ref=proj_out.at[side, slot],
+            send_sem=q_send.at[side * RING + step],
+            recv_sem=q_recv.at[side * RING + slot],
+            device_id=(target, chan),
+            device_id_type=MESH,
+        )
+
+    def term_copy(target, slot):
+        return pltpu.make_async_remote_copy(
+            src_ref=send_t.at[target],
+            dst_ref=token_out.at[slot],
+            send_sem=t_send.at[target],
+            recv_sem=t_recv.at[slot],
+            device_id=(me, target),
+            device_id_type=MESH,
+        )
+
+    def by_token(arrived):
+        arrived = arrived.astype(F32)
+        return jnp.concatenate(
+            [
+                arrived[:, half * CH : (half + 1) * CH, :].reshape(INNER, INNER).T.astype(BF16)
+                for half in range(2)
+            ],
+            axis=0,
+        )
+
+    first_sends = []
+
+    def proj_step(group, i, grads):
+        step = (2, 1, 3, 4)[i]
+        target_plane = lax.rem(plane + step, RING)
+        slab = product(
+            tok_t[pl.ds(pl.multiple_of(target_plane * (RING * depth), 256), RING * depth), :], grads
+        )
+        first, count = GRAD_GROUPS[group]
+        slabs[i, :, first * INNER : (first + count) * INNER] = slab
+        rounded = slab.astype(BF16)
+        for n in range(RING):
+            for j in range(count):
+                cut = rounded[n * depth : (n + 1) * depth, j * INNER : (j + 1) * INNER]
+                send_y[i, n, first + j] = cut[:part]
+                send_z[i, first + j, n] = cut[part:]
+        for n in (2, 1, 3):
+            first_sends.append(y_copy(group, i, lax.rem(row + n, RING), row))
+            first_sends[-1].start()
+        if step < 4:
+            first_sends.append(z_copy(group, i, target_plane, plane))
+            first_sends[-1].start()
+
+    g_arrive()
+    early = by_token(recv_g[:, 0])
+    for i in range(RING):
+        proj_step(0, i, early)
+
     filter_two_grad, filter_one_grad = to_signals(
         [times_conj(spec_grad_two, spec_inner), times_conj(spec_grad_one, spec_values)], bwd, idft, cos, sin
     )
@@ -279,85 +377,15 @@
     own_f = pltpu.make_async_copy(send_f.at[me], sig_out.at[me], own_sem.at[0])
     own_f.start()
 
-    g_arrive()
-    columns = []
-    for n in range(3):
-        arrived = recv_g[:, n].astype(F32)
-        columns.append(
-            jnp.concatenate(
-                [
-                    arrived[:, half * CH : (half + 1) * CH, :].reshape(INNER, INNER).T.astype(BF16)
-                    for half in range(2)
-                ],
-                axis=0,
-            )
-        )
-    grads = jnp.concatenate(columns, axis=1)
-
-    def y_copy(step, target, slot):
-        return pltpu.make_async_remote_copy(
-            src_ref=send_y.at[step, target],
-            dst_ref=recv_y.at[step, slot],
-            send_sem=y_send.at[step * RING + target],
-            recv_sem=y_recv.at[step * RING + slot],
-            device_id=(plane * RING + target, chan),
-            device_id_type=MESH,
-        )
-
-    def z_copy(step, target, slot):
-        return pltpu.make_async_remote_copy(
-            src_ref=send_z.at[step],
-            dst_ref=recv_z.at[slot],
-            send_sem=z_send.at[step],
-            recv_sem=z_recv.at[slot],
-            device_id=(target * RING + row, chan),
-            device_id_type=MESH,
-        )
-
-    def q_copy(side, step, target, slot):
-        return pltpu.make_async_remote_copy(
-            src_ref=send_q.at[side, step],
-            dst_ref=proj_out.at[side, slot],
-            send_sem=q_send.at[side * RING + step],
-            recv_sem=q_recv.at[side * RING + slot],
-            device_id=(target, chan),
-            device_id_type=MESH,
-        )
-
-    def term_copy(target, slot):
-        return pltpu.make_async_remote_copy(
-            src_ref=send_t.at[target],
-            dst_ref=token_out.at[slot],
-            send_sem=t_send.at[target],
-            recv_sem=t_recv.at[slot],
-            device_id=(me, target),
-            device_id_type=MESH,
-        )
-
-    depth = 1024 // SEQ
-    part = depth // 2
-    first_sends = []
+    h_arrive()
+    late = jnp.concatenate([by_token(recv_h[:, n]) for n in range(2)], axis=1)
+    grads = jnp.concatenate([early, late], axis=1)
+
     for i, step in enumerate((2, 1, 3, 4)):
-        target_plane = lax.rem(plane + step, RING)
-        slab = product(
-            tok_t[pl.ds(pl.multiple_of(target_plane * (RING * depth), 256), RING * depth), :], grads
-        )
-        slabs[i] = slab
-        rounded = slab.astype(BF16)
-        for n in range(RING):
-            for j in range(3):
-                cut = rounded[n * depth : (n + 1) * depth, j * INNER : (j + 1) * INNER]
-                send_y[i, n, j] = cut[:part]
-                send_z[i, n, j] = cut[part:]
-        for n in (2, 1, 3):
-            first_sends.append(y_copy(i, lax.rem(row + n, RING), row))
-            first_sends[-1].start()
-        if step < 4:
-            first_sends.append(z_copy(i, target_plane, plane))
-            first_sends[-1].start()
+        proj_step(1, i, late)
         base = lax.rem(chip + step, RING) * 2
         columns = pl.ds(pl.multiple_of(base * INNER, 256), 256)
-        w_rows = jnp.concatenate([weights[j, columns, :] for j in range(3)], axis=1)
+        w_rows = jnp.concatenate([weights[j, columns, :] for j in GRAD_ORDER], axis=1)
         terms = lax.dot_general(grads, w_rows, (((1,), (1,)), ((), ())), preferred_element_type=F32)
         for n in range(2):
             send_t[base + n] = terms[:, n * INNER : (n + 1) * INNER].astype(BF16)
@@ -373,7 +401,8 @@
 
     def sum_y(i):
         for source in rows_y[1:]:
-            y_copy(i, source, source).wait_recv()
+            y_copy(0, i, source, source).wait_recv()
+            y_copy(1, i, source, source).wait_recv()
         mine = slabs[i, pl.ds(pl.multiple_of(row * depth, depth), part), :]
         for j in range(3):
             total = mine[:, j * INNER : (j + 1) * INNER]
@@ -386,14 +415,15 @@
         second_sends.append(q_copy(0, i, planes_z[step] * RING + row, plane))
         second_sends[-1].start()
     for source in planes_z[1:]:
-        z_copy(0, source, source).wait_recv()
+        z_copy(0, 0, source, source).wait_recv()
+        z_copy(1, 0, source, source).wait_recv()
     for n in (2, 1, 3, 0):
         target = rows_y[n]
         mine = slabs[3, pl.ds(pl.multiple_of(target * depth + part, part), part), :]
         for j in range(3):
             total = mine[:, j * INNER : (j + 1) * INNER]
             for source in planes_z[1:]:
-                total += recv_z[source, target, j].astype(F32)
+                total += recv_z[source, j, target].astype(F32)
             send_q[1, n, j] = total.astype(BF16)
         if n > 0:
             second_sends.append(q_copy(1, n, plane * RING + target, row))
@@ -408,7 +438,9 @@
         copy.wait_send()
     a_leave()
     b_leave()
+    c_leave()
     g_leave()
+    h_leave()
     f_arrive()
     f_leave()
 
@@ -439,9 +471,10 @@
     token_grad_ref[...] = sum(token_ref[k].astype(F32) for k in range(CHAN))
     part = proj_ref.shape[3]
     for side in range(2):
-        proj_grad_ref[:, side * part : (side + 1) * part, :] = sum(
-            proj_ref[side, k].astype(F32) for k in range(RING)
-        )
+        for n, j in enumerate(GRAD_ORDER):
+            proj_grad_ref[j, side * part : (side + 1) * part, :] = sum(
+                proj_ref[side, k, n].astype(F32) for k in range(RING)
+            )
 
 
 def shards(tokens, in_proj, filter_one, filter_two, out_grad):
@@ -449,7 +482,7 @@
     depth = in_proj.shape[0]
     anywhere = pl.BlockSpec(memory_space=pl.ANY)
     dma = pltpu.SemaphoreType.DMA
-    block = (SEQ, 3, 2 * CH, INNER)
+    block, two, one = [(SEQ, n, 2 * CH, INNER) for n in (3, 2, 1)]
     fwd, bwd, dft, idft, twiddle = tables()
     arrived = pl.pallas_call(
         chain_kernel,
@@ -472,26 +505,30 @@
             pltpu.VMEM((depth, rows), BF16),
             pltpu.VMEM(block, F32),
             pltpu.VMEM(block, F32),
-            pltpu.VMEM(block, F32),
-            pltpu.VMEM(block, F32),
-            pltpu.VMEM(block, BF16),
-            pltpu.VMEM(block, BF16),
+            pltpu.VMEM(two, F32),
+            pltpu.VMEM(two, F32),
+            pltpu.VMEM(one, F32),
+            pltpu.VMEM(one, F32),
+            pltpu.VMEM(one, BF16),
+            pltpu.VMEM(one, BF16),
+            pltpu.VMEM(two, BF16),
+            pltpu.VMEM(two, BF16),
             pltpu.VMEM(block, BF16),
             pltpu.VMEM((CHAN, rows, width), BF16),
             pltpu.VMEM((RING, depth // RING, 3 * width), F32),
             pltpu.VMEM((RING, RING, 3, depth // SEQ // 2, width), BF16),
             pltpu.VMEM((RING, RING, 3, depth // SEQ // 2, width), BF16),
-            pltpu.VMEM((RING, RING, 3, depth // SEQ // 2, width), BF16),
-            pltpu.VMEM((RING, RING, 3, depth // SEQ // 2, width), BF16),
+            pltpu.VMEM((RING, 3, RING, depth // SEQ // 2, width), BF16),
+            pltpu.VMEM((RING, 3, RING, depth // SEQ // 2, width), BF16),
             pltpu.VMEM((2, RING, 3, depth // SEQ // 2, width), BF16),
             dma((10,)),
             dma((8,)),
             dma((8,)),
         ]
-        + [dma((SEQ,))] * 8
+        + [dma((SEQ,))] * 12
         + [dma((CHAN,))] * 2
-        + [dma((SEQ,))] * 2
-        + [dma((RING,))] * 2
+        + [dma((2 * SEQ,))] * 2
+        + [dma((2 * RING,))] * 2
         + [dma((2 * RING,))] * 2
         + [dma((4,))],
         compiler_params=pltpu.CompilerParams(collective_id=0, has_side_effects=True),

time: 47.1 us -> 47.1 us (level); the launches traced: 46.4 us -> 46.9 us
  Pallas kernels: 45.7 us -> 46.3 us
    pallas_call x1, Pallas kernels: 43.7 us -> 44.2 us  [shards(): pl.pallas_call(chain_kernel, out_shape=(jax.ShapeDtypeStruct(block, BF16)...]
where the time goes in v4:
time: 47.1 us; the launch traced here: 46.9 us
  Pallas kernels  46.3 us (98%)
  between operations  0.64 us (1%)
    pallas_call x1, Pallas kernels, shards(): pl.pallas_call(chain_kernel, out_shape=(jax.ShapeDtypeStruct(block, BF16)...  44.2 us
    pallas_call x1, Pallas kernels, shards(): pl.pallas_call(finish_kernel, out_shape=(flat, flat, jax.ShapeDtypeStruct...  2.06 us

profile of v4, /device:TPU:1, one launch (start us, length us, event | category | flops | bytes accessed | tf_op | source)
XLA Modules:
  0.0 46.9 jit_solution(8917098277104549066)
XLA Ops:
  0.6 44.2 %chain.1 = (bf16[16,3,16,128]{3,2,1,0:T(8,128)(2,1)}, bf16[8,256,128]{2,1,0:T(8,128)(2,1)}, bf16[2,4,3,32,128]{4,3,2,1,0:T(8,128)(2,1)}) custom-call(bf16[256,128]{1,0:T(8,128)(2,1)} %tok_hbm.1, bf16[3,1024,128]{2,1,0:T(8,128)(2,1)} %bitcast.2, f32[256,128]{1,0:T(8,128)} %one_hbm.1, f32[256,128]{1,0:T(8,128)} %two_hbm.1, f32[256,128]{1,0:T(8,128)} %grad_hbm.1, ...), custom_call_target="tpu_custom_call" | custom-call | tf_op jit(solution)/shard_map/chain/pallas_call | solution.py:487
  44.9 2.1 %finish.1 = (f32[256,128]{1,0:T(8,128)}, f32[256,128]{1,0:T(8,128)}, f32[3,64,128]{2,1,0:T(8,128)}, f32[256,128]{1,0:T(8,128)}, f32[256,128]{1,0:T(8,128)}) custom-call(bf16[16,3,16,128]{3,2,1,0:T(8,128)(2,1)} %get-tuple-element.13.sig_ref, bf16[8,256,128]{2,1,0:T(8,128)(2,1)} %get-tuple-element.14.token_ref, ...), custom_call_target="tpu_custom_call" | custom-call | tf_op jit(solution)/shard_map/finish/pallas_call | solution.py:546

commit v5 on v4

--- a/solution.py
+++ b/solution.py
@@ -117,7 +117,7 @@
     slabs, send_y, recv_y, send_z, recv_z, send_q,
     load_sem, tok_send, tok_recv, a_send, a_recv, b_send, b_recv, c_send, c_recv, g_send, g_recv,
     h_send, h_recv, f_send, f_recv,
-    t_send, t_recv, y_send, y_recv, z_send, z_recv, q_send, q_recv, own_sem,
+    t_send, t_recv, y_send, y_recv, z_send, z_recv, q_send, q_recv, own_sem, ready,
 ):
     me = lax.axis_index("seq")
     chan = lax.axis_index("chan")
@@ -148,11 +148,8 @@
 
     barrier = pltpu.get_barrier_semaphore()
 
-    def greet_seq(k, carry):
-        pl.semaphore_signal(
-            barrier, inc=1, device_id=(lax.rem(me + k, SEQ), chan), device_id_type=MESH
-        )
-        return carry
+    beside_y = [(plane * RING + lax.rem(row + k, RING), chan) for k in range(1, RING)]
+    beside_z = [(lax.rem(plane + k, RING) * RING + row, chan) for k in range(1, RING)]
 
     def greet_chan(k, carry):
         pl.semaphore_signal(
@@ -161,13 +158,14 @@
         return carry
 
     lax.fori_loop(1, CHAN, greet_chan, 0)
-    lax.fori_loop(1, SEQ, greet_seq, 0)
+    for target in beside_z + beside_y:
+        pl.semaphore_signal(barrier, inc=1, device_id=target, device_id_type=MESH)
     for n in range(3):
         loads[1 + n].wait()
     for n in range(3):
         for half, block in enumerate(to_blocks(local[n])):
             send_a[:, n, half * CH : (half + 1) * CH, :] = block
-    pl.semaphore_wait(barrier, SEQ + CHAN - 2)
+    pl.semaphore_wait(barrier, CHAN - 1 + 2 * (RING - 1))
 
     def token_copy(source, slot, send, target):
         return pltpu.make_async_remote_copy(
@@ -187,6 +185,8 @@
     own_sends.append(token_copy(tok_hbm, chan, 0, sibling))
     for copy in own_sends:
         copy.start()
+    for target in beside_y:
+        pl.semaphore_signal(ready, inc=1, device_id=target, device_id_type=MESH)
 
     def exchange(send, recv, send_sem, recv_sem):
         def copy(target, slot):
@@ -224,6 +224,7 @@
     h_start, h_arrive, h_leave = exchange(send_h, recv_h, h_send, h_recv)
     f_start, f_arrive, f_leave = exchange(send_f, sig_out, f_send, f_recv)
 
+    pl.semaphore_wait(ready, RING - 1)
     a_start()
     recv_a[me] = send_a[me]
 
@@ -530,7 +531,7 @@
         + [dma((2 * SEQ,))] * 2
         + [dma((2 * RING,))] * 2
         + [dma((2 * RING,))] * 2
-        + [dma((4,))],
+        + [dma((4,)), pltpu.SemaphoreType.REGULAR],
         compiler_params=pltpu.CompilerParams(collective_id=0, has_side_effects=True),
         name="chain",
     )(

time: 47.1 us -> 45.5 us (0.966)
  Pallas kernels: 46.3 us -> 44.7 us
    pallas_call x1, Pallas kernels: 44.2 us -> 42.7 us  [shards(): pl.pallas_call(chain_kernel, out_shape=(jax.ShapeDtypeStruct(block, BF16)...]
where the time goes in v5:
time: 45.5 us; the launch traced here: 45.4 us
  Pallas kernels  44.7 us (98%)
  between operations  0.64 us (1%)
    pallas_call x1, Pallas kernels, shards(): pl.pallas_call(chain_kernel, out_shape=(jax.ShapeDtypeStruct(block, BF16)...  42.7 us
    pallas_call x1, Pallas kernels, shards(): pl.pallas_call(finish_kernel, out_shape=(flat, flat, jax.ShapeDtypeStruct...  2.06 us

profile of v5, /device:TPU:1, one launch (start us, length us, event | category | flops | bytes accessed | tf_op | source)
XLA Modules:
  0.0 45.4 jit_solution(1862456248799830773)
XLA Ops:
  0.6 42.7 %chain.1 = (bf16[16,3,16,128]{3,2,1,0:T(8,128)(2,1)}, bf16[8,256,128]{2,1,0:T(8,128)(2,1)}, bf16[2,4,3,32,128]{4,3,2,1,0:T(8,128)(2,1)}) custom-call(bf16[256,128]{1,0:T(8,128)(2,1)} %tok_hbm.1, bf16[3,1024,128]{2,1,0:T(8,128)(2,1)} %bitcast.2, f32[256,128]{1,0:T(8,128)} %one_hbm.1, f32[256,128]{1,0:T(8,128)} %two_hbm.1, f32[256,128]{1,0:T(8,128)} %grad_hbm.1, ...), custom_call_target="tpu_custom_call" | custom-call | tf_op jit(solution)/shard_map/chain/pallas_call | solution.py:488
  43.3 2.1 %finish.1 = (f32[256,128]{1,0:T(8,128)}, f32[256,128]{1,0:T(8,128)}, f32[3,64,128]{2,1,0:T(8,128)}, f32[256,128]{1,0:T(8,128)}, f32[256,128]{1,0:T(8,128)}) custom-call(bf16[16,3,16,128]{3,2,1,0:T(8,128)(2,1)} %get-tuple-element.13.sig_ref, bf16[8,256,128]{2,1,0:T(8,128)(2,1)} %get-tuple-element.14.token_ref, ...), custom_call_target="tpu_custom_call" | custom-call | tf_op jit(solution)/shard_map/finish/pallas_call | solution.py:547

commit v6 on v5

--- a/solution.py
+++ b/solution.py
@@ -151,21 +151,16 @@
     beside_y = [(plane * RING + lax.rem(row + k, RING), chan) for k in range(1, RING)]
     beside_z = [(lax.rem(plane + k, RING) * RING + row, chan) for k in range(1, RING)]
 
-    def greet_chan(k, carry):
-        pl.semaphore_signal(
-            barrier, inc=1, device_id=(me, lax.rem(chan + k, CHAN)), device_id_type=MESH
-        )
-        return carry
-
-    lax.fori_loop(1, CHAN, greet_chan, 0)
-    for target in beside_z + beside_y:
+    beside_x = [(me, lax.rem(chip + k, RING) * 2 + core) for k in range(1, RING)]
+    beside_x.append((me, chip * 2 + (1 - core)))
+    for target in beside_x + beside_z + beside_y:
         pl.semaphore_signal(barrier, inc=1, device_id=target, device_id_type=MESH)
     for n in range(3):
         loads[1 + n].wait()
     for n in range(3):
         for half, block in enumerate(to_blocks(local[n])):
             send_a[:, n, half * CH : (half + 1) * CH, :] = block
-    pl.semaphore_wait(barrier, CHAN - 1 + 2 * (RING - 1))
+    pl.semaphore_wait(barrier, 1 + 3 * (RING - 1))
 
     def token_copy(source, slot, send, target):
         return pltpu.make_async_remote_copy(

time: 45.5 us -> 46.3 us (1.018)
  Pallas kernels: 44.7 us -> 45.5 us
    pallas_call x1, Pallas kernels: 42.7 us -> 43.4 us  [shards(): pl.pallas_call(chain_kernel, out_shape=(jax.ShapeDtypeStruct(block, BF16)...]
where the time goes in v6:
time: 46.3 us; the launch traced here: 46.1 us
  Pallas kernels  45.5 us (98%)
  between operations  0.64 us (1%)
    pallas_call x1, Pallas kernels, shards(): pl.pallas_call(chain_kernel, out_shape=(jax.ShapeDtypeStruct(block, BF16)...  43.4 us
    pallas_call x1, Pallas kernels, shards(): pl.pallas_call(finish_kernel, out_shape=(flat, flat, jax.ShapeDtypeStruct...  2.06 us

profile of v6, /device:TPU:1, one launch (start us, length us, event | category | flops | bytes accessed | tf_op | source)
XLA Modules:
  0.0 46.1 jit_solution(2859158935447129818)
XLA Ops:
  0.6 43.4 %chain.1 = (bf16[16,3,16,128]{3,2,1,0:T(8,128)(2,1)}, bf16[8,256,128]{2,1,0:T(8,128)(2,1)}, bf16[2,4,3,32,128]{4,3,2,1,0:T(8,128)(2,1)}) custom-call(bf16[256,128]{1,0:T(8,128)(2,1)} %tok_hbm.1, bf16[3,1024,128]{2,1,0:T(8,128)(2,1)} %bitcast.2, f32[256,128]{1,0:T(8,128)} %one_hbm.1, f32[256,128]{1,0:T(8,128)} %two_hbm.1, f32[256,128]{1,0:T(8,128)} %grad_hbm.1, ...), custom_call_target="tpu_custom_call" | custom-call | tf_op jit(solution)/shard_map/chain/pallas_call | solution.py:483
  44.1 2.1 %finish.1 = (f32[256,128]{1,0:T(8,128)}, f32[256,128]{1,0:T(8,128)}, f32[3,64,128]{2,1,0:T(8,128)}, f32[256,128]{1,0:T(8,128)}, f32[256,128]{1,0:T(8,128)}) custom-call(bf16[16,3,16,128]{3,2,1,0:T(8,128)(2,1)} %get-tuple-element.13.sig_ref, bf16[8,256,128]{2,1,0:T(8,128)(2,1)} %get-tuple-element.14.token_ref, ...), custom_call_target="tpu_custom_call" | custom-call | tf_op jit(solution)/shard_map/finish/pallas_call | solution.py:542
